TPU v7x, 128 devices: a whole 4x4x4 slice. The times are simulated.
128 devices in a mesh: row: 16 (over y_hi, x, core), col: 8 (over y_lo, z).
Axes of the slice: x: 4, y: 4 (y_hi: 2, y_lo: 2; y = y_hi * 2 + y_lo), z: 4, core: 2. Of those that a mesh axis runs over, the one named last changes fastest.
Arguments:
- features_t: float32 [18432, 512], P(('row', 'col')), may hold values from -0.0234375 to 0.0234375
- labels: int32 [512], replicated, may hold values from 0 to 1023
- inv_corr: float32 [18432, 18432], P('row', 'col'), may hold values from -1 to 13, as said below
- heads: float32 [18432, 1024], P('row', 'col'), may hold values from -6 to 6
Outputs:
- inv_corr_new: float32 [18432, 18432], P('row', 'col')
- heads_new: float32 [18432, 1024], P('row', 'col')
Inputs may be any that keep to these rules, and one draw needn't show every extreme that they name: inv_corr is symmetric and positive definite, with smallest eigenvalue above 0.5.
All inputs are finite; a program needn't handle non-finite values.
Results may differ from a plain program's by a relative error of at most 0.0001.
Values sent between devices are 32-bit elements; how exact they have to be, the bound alone decides.
A program may use at most 128 MiB of HBM per device.

v0:
```python
import jax
import jax.numpy as jnp
from jax import lax
from jax.sharding import PartitionSpec as P

EXAMPLES = 256


def from_root(value, axis, root):
    mine = lax.axis_index(axis) == root
    return lax.psum(jnp.where(mine, value, jnp.zeros_like(value)), axis)


def in_one(arrays, axis):
    ends = [0]
    for a in arrays:
        ends.append(ends[-1] + a.size)
    subtotal = lax.psum(jnp.concatenate([a.ravel() for a in arrays]), axis)
    return tuple((subtotal[b:e].reshape(a.shape) for a, b, e in zip(arrays, ends, ends[1:])))


def matmul(left, right):
    return jnp.dot(left, right, precision=lax.Precision.HIGHEST, preferred_element_type=jnp.float32)


def contract_rows(left, right):
    return lax.dot_general(
        left,
        right,
        (((0,), (0,)), ((), ())),
        precision=lax.Precision.HIGHEST,
        preferred_element_type=jnp.float32,
    )


def contract_cols(left, right):
    return lax.dot_general(
        left,
        right,
        (((1,), (1,)), ((), ())),
        precision=lax.Precision.HIGHEST,
        preferred_element_type=jnp.float32,
    )


def invert_system(gram):
    identity_mat = jnp.eye(gram.shape[0], dtype=jnp.float32)
    factor = jnp.linalg.cholesky(identity_mat + gram)
    return jax.scipy.linalg.cho_solve((factor, True), identity_mat)


def gather_columns(panel):
    ratio = lax.axis_size("row") // lax.axis_size("col")
    first = ratio * lax.axis_index("col")
    pieces = [from_root(panel, "row", first + member) for member in range(ratio)]
    return jnp.concatenate(pieces, 0)


def row_panel(tile, columns):
    return lax.psum(matmul(tile, columns), "col")


def fitted_terms(rows_part, panel, head):
    return in_one((contract_rows(rows_part, panel), contract_rows(rows_part, head)), "row")


def transposed_panel(rows_part, tile):
    return lax.psum(contract_rows(rows_part, tile), "row")


def on_device(features_t, labels, inv_corr, heads):
    rows_all = lax.all_gather(features_t, "col", axis=0, tiled=True)
    cols_all = gather_columns(rows_all)
    width = heads.shape[1]
    classes = lax.axis_index("col") * width + jnp.arange(width, dtype=jnp.int32)
    targets = (labels[:, None] == classes[None, :]).astype(jnp.float32)
    tile = inv_corr
    head = heads
    panel = row_panel(tile, cols_all)
    gram, fitted = fitted_terms(rows_all, panel, head)
    first_rows = panel[:, :EXAMPLES]
    second_rows = panel[:, EXAMPLES:]
    cross_gram = gram[EXAMPLES:, :EXAMPLES]
    inverse_one = invert_system(gram[:EXAMPLES, :EXAMPLES])
    gain_one = matmul(first_rows, inverse_one)
    linked = matmul(cross_gram, inverse_one)
    panel_two = second_rows - contract_cols(gain_one, cross_gram)
    gram_two = gram[EXAMPLES:, EXAMPLES:] - contract_cols(linked, cross_gram)
    resid_one = targets[:EXAMPLES] - fitted[:EXAMPLES]
    resid_two = targets[EXAMPLES:] - fitted[EXAMPLES:] - matmul(linked, resid_one)
    inverse_two = invert_system(gram_two)
    gain_two = matmul(panel_two, inverse_two)
    head = head + matmul(gain_one, resid_one) + matmul(gain_two, resid_two)
    gains = jnp.concatenate([gain_one, gain_two], 1)
    both_cols = transposed_panel(rows_all, tile)
    second_cols = both_cols[EXAMPLES:] - matmul(linked, both_cols[:EXAMPLES])
    tile = tile - matmul(gains, jnp.concatenate([both_cols[:EXAMPLES], second_cols], 0))
    return (tile, head)


def solution(mesh):
    placed = (P(("row", "col"), None), P(), P("row", "col"), P("row", "col"))
    return jax.shard_map(
        on_device,
        mesh=mesh,
        in_specs=placed,
        out_specs=(P("row", "col"), P("row", "col")),
        check_vma=False,
    )
```

profile of v0, /device:TPU:0, one launch (start us, length us, event | category | flops | bytes accessed | tf_op | source)
XLA Modules:
  0.0 710.2 jit_solution(16788566642092868852)
XLA Ops:
  8.0 46.1 %all-gather.2.cloned.1.call-done = f32[1152,512]{1,0:T(8,128)} async-done(((f32[144,512]{1,0:T(8,128)}), f32[1152,512]{1,0:T(8,128)}) %all-gather.2.cloned.1.call-update) | async-done | bytes 2359312 | tf_op jit(solution)/shard_map/all_gather | solution.py:72
  54.1 4.6 broadcast_select_fusion.1
  58.7 151.6 %all-reduce.11.cloned.1.call-done = (f32[1152,512]{1,0:T(8,128)}, f32[1152,512]{1,0:T(8,128)}) async-done(((f32[1152,512]{1,0:T(8,128)}, f32[1152,512]{1,0:T(8,128)}), (f32[1152,512]{1,0:T(8,128)}, f32[1152,512]{1,0:T(8,128)})) %all-reduce.11.cloned.1.call-update) | async-done | bytes 4718608 | tf_op jit(solution)/shard_map/psum | solution.py:11
  210.3 41.4 %fusion.7 = f32[1152,512]{0,1:T(8,128)} fusion(f32[1152,2304]{1,0:T(8,128)} %param.9, f32[1152,512]{1,0:T(8,128)} %get-tuple-element.38, f32[1152,512]{1,0:T(8,128)} %get-tuple-element.39), kind=kOutput, calls=%fused_computation.14 | convolution fusion | flops 16308633600 | bytes 17694720 | tf_op jit(solution)/shard_map/dot_general | solution.py:23
  253.4 4.6 convolution_bitcast_fusion
  258.0 23.0 %fusion.61 = f32[512,2304]{1,0:T(8,128)} fusion(f32[1152,512]{1,0:T(8,128)S(1)} %copy-done, f32[1152,2304]{1,0:T(8,128)} %param.9), kind=kOutput, calls=%fused_computation.111 | convolution fusion | flops 16307453952 | bytes 17694720 | tf_op jit(solution)/shard_map/dot_general | solution.py:27
  281.0 56.0 %all-reduce.7.cloned.1.call-done = f32[1152,512]{0,1:T(8,128)} async-done(((f32[1152,512]{0,1:T(8,128)}), f32[1152,512]{0,1:T(8,128)}) %all-reduce.7.cloned.1.call-update) | async-done | bytes 2359312 | tf_op jit(solution)/shard_map/psum | solution.py:60
  337.0 6.0 convolution_bitcast_fusion.1
  346.7 154.9 %all-reduce.9.cloned.1.call-done = (f32[327680]{0:T(1024)}, f32[512,2304]{1,0:T(8,128)}) async-done(((f32[327680]{0:T(1024)}, f32[512,2304]{1,0:T(8,128)}), (f32[327680]{0:T(1024)}, f32[512,2304]{1,0:T(8,128)})) %all-reduce.9.cloned.1.call-update) | async-done | bytes 6029328 | tf_op jit(solution)/shard_map/psum | solution.py:18
  504.3 11.7 %cholesky.130 = f32[128,128]{1,0:T(8,128)S(1)} custom-call(f32[128,128]{1,0:T(8,128)S(1)} %cholesky.194), custom_call_target="Cholesky" | custom-call | tf_op jit(solution)/shard_map/jit(cholesky)/cholesky | solution.py:48
  516.1 9.8 %custom-call.15 = f32[1,128,128]{1,2,0:T(8,128)S(1)} custom-call(f32[1,128,128]{2,1,0:T(8,128)S(1)} %get-tuple-element.55), custom_call_target="InvertDiagBlocksLowerTriangular" | custom-call | tf_op jit(solution)/shard_map/jit(cholesky)/cholesky | solution.py:48
  526.4 11.9 %cholesky.147 = f32[128,128]{1,0:T(8,128)S(1)} custom-call(f32[128,128]{1,0:T(8,128)S(1)} %convolution_subtract_fusion.10), custom_call_target="Cholesky" | custom-call | tf_op jit(solution)/shard_map/jit(cholesky)/cholesky | solution.py:48
  540.5 4.1 while.4
  544.6 19.7 %custom-call.16 = f32[2,128,128]{1,2,0:T(8,128)S(1)} custom-call(f32[2,128,128]{2,1,0:T(8,128)S(1)} %get-tuple-element.18), custom_call_target="InvertDiagBlocksLowerTriangular" | custom-call | tf_op jit(solution)/shard_map/jit(_cho_solve)/triangular_solve | solution.py:49
  566.9 1.8 slice.153
  568.7 5.9 convolution_subtract_fusion.1
  575.8 2.0 convolution_subtract_fusion.4
  577.9 1.8 copy.14
  582.1 13.2 %cholesky.164 = f32[128,128]{1,0:T(8,128)} custom-call(f32[128,128]{1,0:T(8,128)} %cholesky.197), custom_call_target="Cholesky" | custom-call | tf_op jit(solution)/shard_map/jit(cholesky)/cholesky | solution.py:48
  597.5 11.3 %custom-call.17 = f32[1,128,128]{1,2,0:T(8,128)} custom-call(f32[1,128,128]{2,1,0:T(8,128)} %get-tuple-element.51), custom_call_target="InvertDiagBlocksLowerTriangular" | custom-call | tf_op jit(solution)/shard_map/jit(cholesky)/cholesky | solution.py:48
  610.3 1.7 constant_dynamic-update-slice_fusion.1
  612.0 1.7 convolution_subtract_fusion.9
  613.8 13.6 %cholesky.181 = f32[128,128]{1,0:T(8,128)} custom-call(f32[128,128]{1,0:T(8,128)} %convolution_subtract_fusion.9), custom_call_target="Cholesky" | custom-call | tf_op jit(solution)/shard_map/jit(cholesky)/cholesky | solution.py:48
  630.9 1.7 select_select_fusion
  633.3 7.0 while.5
  633.9 2.9 bitcast_dynamic-update-slice_fusion.5
  637.4 2.8 bitcast_dynamic-update-slice_fusion.5
  640.2 21.1 %custom-call.18 = f32[2,128,128]{1,2,0:T(8,128)} custom-call(f32[2,128,128]{2,1,0:T(8,128)} %get-tuple-element.19), custom_call_target="InvertDiagBlocksLowerTriangular" | custom-call | tf_op jit(solution)/shard_map/jit(_cho_solve)/triangular_solve | solution.py:49
  668.6 2.7 fusion.13
  671.3 3.0 convolution_add_fusion.1
  677.0 2.9 convolution_add_fusion
  679.9 23.6 %convolution_subtract_fusion = f32[1152,2304]{1,0:T(8,128)} fusion(f32[1152,2304]{1,0:T(8,128)} %param.9, f32[256,2304]{1,0:T(8,128)S(1)} %copy-done.1, f32[256,2304]{1,0:T(8,128)S(1)} %slice.153, f32[1152,256]{0,1:T(8,128)S(1)} %fusion.16, f32[1152,256]{0,1:T(8,128)S(1)} %fusion.13), kind=kOutput, calls=%fused_computation.4 | convolution fusion | flops 16311877632 | bytes 28311552 | tf_op jit(solution)/shard_map/dot_general | solution.py:23
  (95 shorter events, 38.0 us)
Async XLA Ops:
  7.2 46.9 %all-gather.2.cloned.1.call-start = ((), (), s32[]{:S(2)}) async-start(), calls=%async_computation | async-start | bytes 2654208 | tf_op jit(solution)/shard_map/all_gather | solution.py:72
  7.9 202.4 %all-reduce.11.cloned.1.call-start = ((), (), s32[]{:S(2)}) async-start(), calls=%async_computation.3 | async-start | bytes 9437184 | tf_op jit(solution)/shard_map/psum | solution.py:11
  58.7 278.3 %all-reduce.7.cloned.1.call-start = ((), (), s32[]{:S(2)}) async-start(), calls=%async_computation.1 | async-start | bytes 4718592 | tf_op jit(solution)/shard_map/psum | solution.py:60
  210.3 41.5 %copy-start.4 = (f32[1152,128]{1,0:T(8,128)S(1)}, f32[1152,128]{1,0:T(8,128)}, u32[]{:S(2)}) copy-start(f32[1152,128]{1,0:T(8,128)} %param.10) | copy-start | bytes 1769476
  251.7 1.7 copy-start
  251.8 249.8 %all-reduce.9.cloned.1.call-start = ((), (), s32[]{:S(2)}) async-start(), calls=%async_computation.2 | async-start | bytes 12058624 | tf_op jit(solution)/shard_map/psum | solution.py:18
  343.0 1.0 copy-start.7
  345.2 0.7 copy-start.13
  345.8 218.8 %copy-start.3 = (f32[256,256]{0,1:T(8,128)}, f32[256,256]{0,1:T(8,128)S(1)}, u32[]{:S(2)}) copy-start(f32[256,256]{0,1:T(8,128)S(1)} %fusion.22) | copy-start | bytes 786436
  566.2 0.7 copy-start.6
  568.7 6.0 copy-start.10
  568.7 7.1 %copy-start.8 = (f32[512,128]{1,0:T(8,128)S(1)}, f32[512,128]{1,0:T(8,128)}, u32[]{:S(2)}) copy-start(f32[512,128]{1,0:T(8,128)} %compare_convert_fusion) | copy-start | bytes 786436
  580.7 0.8 copy-start.11
  661.3 10.0 %copy-start.5 = (f32[1152,128]{1,0:T(8,128)S(1)}, f32[1152,128]{1,0:T(8,128)}, u32[]{:S(2)}) copy-start(f32[1152,128]{1,0:T(8,128)} %param.10) | copy-start | bytes 1769476
  661.3 10.0 %copy-start.9 = (f32[512,128]{1,0:T(8,128)S(1)}, f32[512,128]{1,0:T(8,128)}, u32[]{:S(2)}) copy-start(f32[512,128]{1,0:T(8,128)} %compare_convert_fusion) | copy-start | bytes 786436
  668.5 5.8 copy-start.2
  674.3 2.7 copy-start.12
  675.6 4.2 copy-start.1
Sparse Core Ops, SparseCore 0:
  9.6 44.3 all-gather.1
  58.8 151.4 all-reduce.10
  251.9 85.0 all-reduce.6
  345.3 156.2 all-reduce.8
where the time goes:
time: 721 us; the launch traced here: 710 us
  waiting for transfers between devices  409 us (57%)
  matrix products  132 us (18%)
  other arithmetic  127 us (18%)
  local copies, waits for them, and re-layouts  24.4 us (3%)
  between operations  17.1 us (2%)
    psum x1, waiting for transfers between devices, in_one(): subtotal = lax.psum(jnp.concatenate([a.ravel() for a in arrays]), axis)  155 us
    psum x1, waiting for transfers between devices, from_root(): return lax.psum(jnp.where(mine, value, jnp.zeros_like(value)), axis)  152 us
    dot_general x9, matrix products, matmul(): jnp.dot(left, right, precision=lax.Precision.HIGHEST, preferred_element_t...  83.2 us
    another operation x13, other arithmetic, invert_system(): factor = jnp.linalg.cholesky(identity_mat + gram)  76.6 us
    psum x1, waiting for transfers between devices, row_panel(): return lax.psum(matmul(tile, columns), 'col')  56 us
    all_gather x1, waiting for transfers between devices, on_device(): rows_all = lax.all_gather(features_t, 'col', axis=0, tiled=True)  46.1 us
    another operation x5, other arithmetic, invert_system(): return jax.scipy.linalg.cho_solve((factor, True), identity_mat)  42.5 us
    dot_general x3, matrix products, contract_rows(): lax.dot_general(left, right, (((0,), (0,)), ((), ())), precision=lax.Prec...  33.5 us
  transfers between devices with their start and end apart: 4, of which 4 were waited for; matrix products, arithmetic and copies ran while one was open for 4% of the time, Pallas kernels for 0%

commit v1 on v0

v1 whole, which is shorter than its diff:
```python
import jax
import jax.numpy as jnp
from jax import lax
from jax.experimental import pallas as pl
from jax.experimental.pallas import tpu as pltpu
from jax.sharding import PartitionSpec as P

F32 = jnp.float32
BF16 = jnp.bfloat16
MESH = pl.DeviceIdType.MESH
ALL = 512
CHUNK = 64
MIB = 1 << 20


def split(value):
    hi = value.astype(BF16)
    lo = (value - hi.astype(F32)).astype(BF16)
    return hi, lo


def mm(left, right):
    return jnp.dot(left, right, preferred_element_type=F32)


def dot3(left, right):
    (lh, ll), (rh, rl) = left, right
    return mm(lh, rh) + (mm(lh, rl) + mm(ll, rh))


class Place:
    def __init__(self):
        self.row, self.col = row, col = lax.axis_index("row"), lax.axis_index("col")
        self.core = core = lax.rem(row, 2)
        self.chip_row = chip_row = row // 2
        self.y_hi, self.x = y_hi, x = chip_row // 4, lax.rem(chip_row, 4)
        self.y_lo, self.z = y_lo, z = col // 4, lax.rem(col, 4)
        self.sibling = (chip_row * 2 + (1 - core), col)
        self.x_up = ((y_hi * 4 + lax.rem(x + 1, 4)) * 2 + core, col)
        self.x_down = ((y_hi * 4 + lax.rem(x + 3, 4)) * 2 + core, col)
        self.x_far = ((y_hi * 4 + lax.rem(x + 2, 4)) * 2 + core, col)
        self.y_far = (((1 - y_hi) * 4 + x) * 2 + core, col)
        self.z_up = (row, y_lo * 4 + lax.rem(z + 1, 4))
        self.z_down = (row, y_lo * 4 + lax.rem(z + 3, 4))
        self.y_near = (row, (1 - y_lo) * 4 + z)
        self.swapped = (col * 2 + core, chip_row)


class Copies:
    def __init__(self, send_sems, recv_sems):
        self.send_sems, self.recv_sems = send_sems, recv_sems
        self.count = 0
        self.started = []

    def take(self):
        self.count += 1
        return self.count - 1

    def make(self, index, src, dst, device):
        return pltpu.make_async_remote_copy(
            src_ref=src, dst_ref=dst, send_sem=self.send_sems.at[index], recv_sem=self.recv_sems.at[index],
            device_id=device, device_id_type=MESH)

    def start(self, src, dst, device):
        index = self.take()
        copy = self.make(index, src, dst, device)
        copy.start()
        self.started.append(copy)
        return index

    def arrived(self, index, landing, device):
        self.make(index, landing, landing, device).wait_recv()

    def finish(self):
        for copy in self.started:
            copy.wait_send()


def greet(devices):
    barrier = pltpu.get_barrier_semaphore()
    for device in devices:
        pl.semaphore_signal(barrier, inc=1, device_id=device, device_id_type=MESH)
    pl.semaphore_wait(barrier, len(devices))


class Gather:
    def __init__(self, copies, buf, pair_at, ring_at, pair, up, down, rows):
        self.c, self.buf, self.rows = copies, buf, rows
        self.a, self.b = pair_at, ring_at
        self.pair, self.up, self.down = pair, up, down

    def slot(self, pair_step, ring_step):
        a = self.a if pair_step == 0 else 1 - self.a
        return a * 4 + lax.rem(self.b + ring_step, 4)

    def part(self, pair_step, ring_step, half=None):
        at = self.slot(pair_step, ring_step)
        if half is None:
            return self.buf.at[at]
        n = self.rows // 2
        return self.buf.at[at, pl.ds(half * n, n)]

    def same(self, part, device):
        return self.c.start(part, part, device)

    def own(self):
        mine = self.part(0, 0)
        self.i_up = self.same(mine, self.up)
        self.i_down = self.same(mine, self.down)
        self.i_pair = self.same(mine, self.pair)

    def forward_own(self):
        self.c.arrived(self.i_up, self.part(0, 3), self.down)
        self.h_up = self.same(self.part(0, 3, 0), self.up)
        self.c.arrived(self.i_down, self.part(0, 1), self.up)
        self.h_down = self.same(self.part(0, 1, 1), self.down)

    def pair_across(self):
        self.c.arrived(self.i_pair, self.part(1, 0), self.pair)
        self.q_up = self.same(self.part(1, 0), self.up)
        self.q_down = self.same(self.part(1, 0), self.down)

    def far_own(self):
        self.c.arrived(self.h_up, self.part(0, 2, 0), self.down)
        self.c.arrived(self.h_down, self.part(0, 2, 1), self.up)

    def far_by_pair(self):
        self.f_pair = self.same(self.part(0, 2), self.pair)

    def end_by_pair(self):
        self.c.arrived(self.q_up, self.part(1, 3), self.down)
        self.c.arrived(self.q_down, self.part(1, 1), self.up)
        self.c.arrived(self.f_pair, self.part(1, 2), self.pair)

    def forward_pair(self):
        self.c.arrived(self.q_up, self.part(1, 3), self.down)
        self.g_up = self.same(self.part(1, 3, 0), self.up)
        self.c.arrived(self.q_down, self.part(1, 1), self.up)
        self.g_down = self.same(self.part(1, 1, 1), self.down)

    def end_by_ring(self):
        self.c.arrived(self.g_up, self.part(1, 2, 0), self.down)
        self.c.arrived(self.g_down, self.part(1, 2, 1), self.up)


def gather_kernel(x_ref, out_ref, local_sem, send_sems, recv_sems):
    at = Place()
    mine = pltpu.make_async_copy(x_ref, out_ref.at[at.col], local_sem)
    mine.start()
    greet([at.y_near, at.z_up, at.z_down])
    mine.wait()
    copies = Copies(send_sems, recv_sems)
    g = Gather(copies, out_ref, at.y_lo, at.z, at.y_near, at.z_up, at.z_down, x_ref.shape[0])
    g.own()
    g.forward_own()
    g.pair_across()
    g.far_own()
    g.far_by_pair()
    g.end_by_pair()
    copies.finish()


def gather_rows(features_t):
    rows, examples = features_t.shape
    out = pl.pallas_call(
        gather_kernel,
        out_shape=jax.ShapeDtypeStruct((8, rows, examples), F32),
        in_specs=[pl.BlockSpec(memory_space=pltpu.VMEM)],
        out_specs=pl.BlockSpec(memory_space=pltpu.VMEM),
        scratch_shapes=[pltpu.SemaphoreType.DMA, pltpu.SemaphoreType.DMA((8,)), pltpu.SemaphoreType.DMA((8,))],
        compiler_params=pltpu.CompilerParams(collective_id=0, has_side_effects=True, vmem_limit_bytes=48 * MIB),
        name="gather_rows",
    )(features_t)
    return out.reshape(8 * rows, examples)


def partial_kernel(x_ref, r_ref, w_ref, p_ref, f_ref, xh_ref, xl_ref):
    @pl.when((pl.program_id(0) == 0) & (pl.program_id(1) == 0))
    def _():
        xh, xl = split(x_ref[...].T)
        xh_ref[...] = xh
        xl_ref[...] = xl
        f_ref[...] = dot3((xh, xl), split(w_ref[...]))

    p_ref[0] = dot3((xh_ref[...], xl_ref[...]), split(r_ref[...]))


def partial_panel(x_rows, tile, head):
    rows, examples = x_rows.shape
    width = tile.shape[1] // 2
    block = width // 3
    return pl.pallas_call(
        partial_kernel,
        grid=(2, 3),
        out_shape=(jax.ShapeDtypeStruct((2, examples, width), F32), jax.ShapeDtypeStruct((examples, head.shape[1]), F32)),
        in_specs=[
            pl.BlockSpec((rows, examples), lambda h, j: (0, 0)),
            pl.BlockSpec((rows, block), lambda h, j: (0, h * 3 + j)),
            pl.BlockSpec(head.shape, lambda h, j: (0, 0)),
        ],
        out_specs=(
            pl.BlockSpec((1, examples, block), lambda h, j: (h, 0, j)),
            pl.BlockSpec((examples, head.shape[1]), lambda h, j: (0, 0)),
        ),
        scratch_shapes=[pltpu.VMEM((examples, rows), BF16), pltpu.VMEM((examples, rows), BF16)],
        compiler_params=pltpu.CompilerParams(vmem_limit_bytes=48 * MIB),
        name="partial_panel",
    )(x_rows, tile, head)


def panels_kernel(p_ref, x_ref, uc_ref, ur_ref, s_ref, from_sib, acc, ra, rb, ry, sp, rs0, sh, rs1, sh2, rs2,
                  send_sems, recv_sems):
    at = Place()
    k, p, col = at.core, at.chip_row, at.col
    barrier = pltpu.get_barrier_semaphore()
    near = [at.sibling, at.x_up, at.x_down, at.x_far, at.y_far, at.z_up, at.z_down, at.y_near]
    for device in near:
        pl.semaphore_signal(barrier, inc=1, device_id=device, device_id_type=MESH)
    off_diagonal = p != col

    @pl.when(off_diagonal)
    def _():
        pl.semaphore_signal(barrier, inc=1, device_id=at.swapped, device_id_type=MESH)
        pl.semaphore_wait(barrier, len(near) + 1)

    @pl.when(jnp.logical_not(off_diagonal))
    def _():
        pl.semaphore_wait(barrier, len(near))

    copies = Copies(send_sems, recv_sems)

    def chunk(y_step, x_step):
        y = at.y_hi if y_step == 0 else 1 - at.y_hi
        return y * 4 + lax.rem(at.x + x_step, 4)

    order = [(1, 2), (0, 2), (1, 1), (0, 1), (1, 3), (0, 3), (1, 0), (0, 0)]
    sib = {}
    for step in order:
        ch = chunk(*step)
        sib[step] = copies.start(p_ref.at[1 - k, ch], from_sib.at[ch], at.sibling)

    def add_sibling(step):
        ch = chunk(*step)
        copies.arrived(sib[step], from_sib.at[ch], at.sibling)
        acc[ch] = p_ref[k, ch] + from_sib[ch]

    half = CHUNK // 2
    low, high = pl.ds(0, half), pl.ds(half, half)
    a_up, a_down, b_up, b_down = {}, {}, {}, {}
    for y in (1, 0):
        add_sibling((y, 2))
        ch = chunk(y, 2)
        a_up[y] = copies.start(acc.at[ch, low], ra.at[0, y], at.x_up)
        a_down[y] = copies.start(acc.at[ch, high], ra.at[1, y], at.x_down)
    for y in (1, 0):
        add_sibling((y, 1))
        add_sibling((y, 3))
    for y in (1, 0):
        ch = chunk(y, 1)
        copies.arrived(a_up[y], ra.at[0, y], at.x_down)
        acc[ch, low] = acc[ch, low] + ra[0, y]
        b_up[y] = copies.start(acc.at[ch], rb.at[0, y], at.x_up)
        ch = chunk(y, 3)
        copies.arrived(a_down[y], ra.at[1, y], at.x_up)
        acc[ch, high] = acc[ch, high] + ra[1, y]
        b_down[y] = copies.start(acc.at[ch], rb.at[1, y], at.x_down)
    add_sibling((1, 0))
    add_sibling((0, 0))

    def add_x(y):
        ch = chunk(y, 0)
        copies.arrived(b_up[y], rb.at[0, y], at.x_down)
        copies.arrived(b_down[y], rb.at[1, y], at.x_up)
        return acc[ch] + (rb[0, y] + rb[1, y])

    ch = chunk(1, 0)
    acc[ch] = add_x(1)
    c_far = copies.start(acc.at[ch], ry, at.y_far)
    mine = add_x(0)
    copies.arrived(c_far, ry, at.y_far)
    uc_ref[k, p] = mine + ry[...]

    own_block = uc_ref.at[k]
    t = copies.take()
    swap = copies.make(t, uc_ref.at[k, p], ur_ref.at[p], at.swapped)

    @pl.when(off_diagonal)
    def _():
        swap.start()

    gc = Gather(copies, own_block, at.y_hi, at.x, at.y_far, at.x_up, at.x_down, CHUNK)
    gr = Gather(copies, ur_ref, at.y_lo, at.z, at.y_near, at.z_up, at.z_down, CHUNK)
    gc.own()

    @pl.when(off_diagonal)
    def _():
        copies.make(t, ur_ref.at[col], ur_ref.at[col], at.swapped).wait_recv()
        swap.wait_send()

    @pl.when(jnp.logical_not(off_diagonal))
    def _():
        ur_ref[col] = uc_ref[k, p]

    gr.own()
    sp[...] = dot3(split(ur_ref[col]), split(x_ref[...]))
    s0 = copies.start(sp.at[pl.ds((1 - k) * half, half)], rs0, at.sibling)
    gc.forward_own()
    copies.arrived(s0, rs0, at.sibling)
    sh[...] = sp[pl.ds(pl.multiple_of(k * half, half), half)] + rs0[...]
    s1 = [copies.start(sh, rs1.at[i], d) for i, d in enumerate((at.x_up, at.x_down, at.x_far))]
    gc.pair_across()
    gr.forward_own()
    gr.pair_across()
    for i, d in enumerate((at.x_down, at.x_up, at.x_far)):
        copies.arrived(s1[i], rs1.at[i], d)
    sh2[...] = sh[...] + rs1[0] + (rs1[1] + rs1[2])
    s2 = copies.start(sh2, rs2, at.y_far)
    copies.arrived(s2, rs2, at.y_far)
    s_ref[k, col] = sh2[...] + rs2[...]
    gs = Gather(copies, s_ref.at[k], at.y_lo, at.z, at.y_near, at.z_up, at.z_down, half)
    gs.own()
    gs.forward_own()
    gs.pair_across()
    gs.far_own()
    gs.forward_pair()
    gs.end_by_ring()
    s4 = copies.start(s_ref.at[k], s_ref.at[k], at.sibling)

    gc.far_own()
    gc.forward_pair()
    gr.far_own()
    gr.forward_pair()
    gc.end_by_ring()
    u4 = copies.start(own_block, own_block, at.sibling)
    gr.end_by_ring()
    copies.arrived(s4, s_ref.at[1 - k], at.sibling)
    copies.arrived(u4, uc_ref.at[1 - k], at.sibling)
    copies.finish()


def panels(partial, x_rows):
    width = partial.shape[2]
    half = CHUNK // 2
    vmem = pl.BlockSpec(memory_space=pltpu.VMEM)
    return pl.pallas_call(
        panels_kernel,
        out_shape=(
            jax.ShapeDtypeStruct((2, 8, CHUNK, width), F32),
            jax.ShapeDtypeStruct((8, CHUNK, width), F32),
            jax.ShapeDtypeStruct((2, 8, half, ALL), F32),
        ),
        in_specs=[vmem] * 2,
        out_specs=(vmem,) * 3,
        scratch_shapes=[
            pltpu.VMEM((8, CHUNK, width), F32),
            pltpu.VMEM((8, CHUNK, width), F32),
            pltpu.VMEM((2, 2, half, width), F32),
            pltpu.VMEM((2, 2, CHUNK, width), F32),
            pltpu.VMEM((CHUNK, width), F32),
            pltpu.VMEM((CHUNK, ALL), F32),
            pltpu.VMEM((half, ALL), F32),
            pltpu.VMEM((half, ALL), F32),
            pltpu.VMEM((3, half, ALL), F32),
            pltpu.VMEM((half, ALL), F32),
            pltpu.VMEM((half, ALL), F32),
            pltpu.SemaphoreType.DMA((64,)),
            pltpu.SemaphoreType.DMA((64,)),
        ],
        compiler_params=pltpu.CompilerParams(collective_id=1, has_side_effects=True, vmem_limit_bytes=48 * MIB),
        name="panels",
    )(partial.reshape(2, 8, CHUNK, width), x_rows)


def inverse_kernel(s_ref, ur_ref, mh_ref, ml_ref, a_ref, g_ref):
    half = CHUNK // 2
    for c in range(8):
        for k in range(2):
            a_ref[pl.ds(c * CHUNK + k * half, half)] = s_ref[k, c]
    rows = lax.broadcasted_iota(jnp.int32, (ALL, ALL), 0)
    cols = lax.broadcasted_iota(jnp.int32, (ALL, ALL), 1)
    eye = jnp.where(rows == cols, 1.0, 0.0).astype(F32)
    a_ref[...] = a_ref[...] + eye
    bound = jnp.max(jnp.sum(jnp.abs(a_ref[...]), axis=0, keepdims=True))
    scale = 2.0 / (1.0 + bound)
    g_ref[...] = scale * (2.0 * eye - scale * a_ref[...])

    def more(state):
        step, size = state
        return (step < 60) & (size > 1e-7)

    def refine(state):
        step, _ = state
        g = g_ref[...]
        error = eye - jnp.dot(a_ref[...], g, precision=lax.Precision.HIGHEST, preferred_element_type=F32)
        g_ref[...] = g + dot3(split(g), split(error))
        return step + 1, jnp.sum(error * error)

    lax.while_loop(more, refine, (jnp.int32(0), F32(1.0)))
    mh, ml = split(dot3(split(ur_ref[...].T), split(g_ref[...])))
    mh_ref[...] = mh
    ml_ref[...] = ml


def gain_of(gram, rows_t):
    width = rows_t.shape[1]
    vmem = pl.BlockSpec(memory_space=pltpu.VMEM)
    return pl.pallas_call(
        inverse_kernel,
        out_shape=(jax.ShapeDtypeStruct((width, ALL), BF16),) * 2,
        in_specs=[vmem] * 2,
        out_specs=(vmem,) * 2,
        scratch_shapes=[pltpu.VMEM((ALL, ALL), F32), pltpu.VMEM((ALL, ALL), F32)],
        compiler_params=pltpu.CompilerParams(vmem_limit_bytes=48 * MIB),
        name="gain",
    )(gram, rows_t)


def update_kernel(mh_ref, ml_ref, u_ref, r_ref, resid_ref, w_ref, out_ref, head_ref):
    gain = (mh_ref[...], ml_ref[...])

    @pl.when((pl.program_id(0) == 0) & (pl.program_id(1) == 0))
    def _():
        head_ref[...] = w_ref[...] + dot3(gain, split(resid_ref[...]))

    out_ref[...] = r_ref[...] - dot3(gain, split(u_ref[0]))


def update(gain_hi, gain_lo, cols_t, tile, resid, head):
    rows = tile.shape[0]
    width = tile.shape[1] // 2
    block = width // 3
    whole = lambda h, j: (0, 0)
    return pl.pallas_call(
        update_kernel,
        grid=(2, 3),
        out_shape=(jax.ShapeDtypeStruct(tile.shape, F32), jax.ShapeDtypeStruct(head.shape, F32)),
        in_specs=[
            pl.BlockSpec((rows, ALL), whole),
            pl.BlockSpec((rows, ALL), whole),
            pl.BlockSpec((1, ALL, block), lambda h, j: (h, 0, j)),
            pl.BlockSpec((rows, block), lambda h, j: (0, h * 3 + j)),
            pl.BlockSpec(resid.shape, whole),
            pl.BlockSpec(head.shape, whole),
        ],
        out_specs=(pl.BlockSpec((rows, block), lambda h, j: (0, h * 3 + j)), pl.BlockSpec(head.shape, whole)),
        compiler_params=pltpu.CompilerParams(vmem_limit_bytes=48 * MIB),
        name="update",
    )(gain_hi, gain_lo, cols_t, tile, resid, head)


def on_device(features_t, labels, inv_corr, heads):
    width = heads.shape[1]
    classes = lax.axis_index("col") * width + jnp.arange(width, dtype=jnp.int32)
    targets = (labels[:, None] == classes[None, :]).astype(F32)
    x_rows = gather_rows(features_t)
    partial, fitted = partial_panel(x_rows, inv_corr, heads)
    resid = targets - lax.psum(fitted, "row")
    cols_t, rows_t, gram = panels(partial, x_rows)
    block = partial.shape[2]
    gain_hi, gain_lo = gain_of(gram, rows_t.reshape(ALL, block))
    return update(gain_hi, gain_lo, cols_t.reshape(2, ALL, block), inv_corr, resid, heads)


def solution(mesh):
    placed = (P(("row", "col"), None), P(), P("row", "col"), P("row", "col"))
    return jax.shard_map(
        on_device,
        mesh=mesh,
        in_specs=placed,
        out_specs=(P("row", "col"), P("row", "col")),
        check_vma=False,
    )
```

time: 721 us -> 226 us (0.31); the launches traced: 710 us -> 225 us
  waiting for transfers between devices: 409 us -> 21.4 us
  Pallas kernels: 0 us -> 181 us
  matrix products: 132 us -> 0 us
  other arithmetic: 127 us -> 1.09 us
  local copies, waits for them, and re-layouts: 24.4 us -> 7.31 us
    psum x3 -> x1, waiting for transfers between devices: 363 us -> 21.4 us  [on_device(): resid = targets - lax.psum(fitted, 'row')]
    pallas_call x0 -> x5, Pallas kernels: none -> 181 us  [the longest x1 103 us: panels(): pl.pallas_call(panels_kernel, out_shape=(jax.ShapeDtypeStruct((2, 8, CHUN...]
    dot_general x14 -> x0, matrix products: 119 us -> none  [the longest x9 83.2 us: matmul(): jnp.dot(left, right, precision=lax.Precision.HIGHEST, preferred_element_t...]
    another operation x18 -> x0, other arithmetic: 119 us -> none  [the longest x13 76.6 us: invert_system(): factor = jnp.linalg.cholesky(identity_mat + gram)]
    all_gather x1 -> x0, waiting for transfers between devices: 46.1 us -> none  [on_device(): rows_all = lax.all_gather(features_t, 'col', axis=0, tiled=True)]
    another operation x19 -> x0, local copies, waits for them, and re-layouts: 14 us -> none  [the longest x15 11.8 us: invert_system(): return jax.scipy.linalg.cho_solve((factor, True), identity_mat)]
    another operation x16 -> x0, matrix products: 12.9 us -> none  [the longest x12 9.01 us: invert_system(): return jax.scipy.linalg.cho_solve((factor, True), identity_mat)]
  transfers between devices with their start and end apart: 4 -> 1, of which waited for: 4 -> 1; matrix products, arithmetic and copies ran while one was open for 4% -> 0% of each run, Pallas kernels for 0% -> 55%
where the time goes in v1:
time: 226 us; the launch traced here: 225 us
  Pallas kernels  181 us (80%)
  waiting for transfers between devices  21.4 us (9%)
  between operations  14.1 us (6%)
  local copies, waits for them, and re-layouts  7.31 us (3%)
    pallas_call x1, Pallas kernels, panels(): pl.pallas_call(panels_kernel, out_shape=(jax.ShapeDtypeStruct((2, 8, CHUN...  103 us
    pallas_call x1, Pallas kernels, gather_rows(): pl.pallas_call(gather_kernel, out_shape=jax.ShapeDtypeStruct((8, rows, ex...  24.1 us
    psum x1, waiting for transfers between devices, on_device(): resid = targets - lax.psum(fitted, 'row')  21.4 us
    pallas_call x1, Pallas kernels, gain_of(): pl.pallas_call(inverse_kernel, out_shape=(jax.ShapeDtypeStruct((width, AL...  19.8 us
    pallas_call x1, Pallas kernels, update(): pl.pallas_call(update_kernel, grid=(2, 3), out_shape=(jax.ShapeDtypeStruc...  17.5 us
    pallas_call x1, Pallas kernels, partial_panel(): pl.pallas_call(partial_kernel, grid=(2, 3), out_shape=(jax.ShapeDtypeStru...  16.6 us
    unnamed x16, local copies, waits for them, and re-layouts  7.31 us
  transfers between devices with their start and end apart: 1, of which 1 were waited for; matrix products, arithmetic and copies ran while one was open for 0% of the time, Pallas kernels for 55%

profile of v1, /device:TPU:0, one launch (start us, length us, event | category | flops | bytes accessed | tf_op | source)
XLA Modules:
  0.0 224.9 jit_solution(8664512837193041664)
XLA Ops:
  7.2 0.0 all-reduce.2.cloned.1.call-start
  7.2 0.0 copy-start.6
  7.2 1.0 copy-done.6
  8.2 24.1 %gather_rows.1 = f32[8,144,512]{2,1,0:T(8,128)S(1)} custom-call(f32[144,512]{1,0:T(8,128)S(1)} %copy-done.6), custom_call_target="tpu_custom_call" | custom-call | tf_op jit(solution)/shard_map/gather_rows/pallas_call | solution.py:165
  32.3 0.0 copy-start
  32.3 1.1 copy-done
  33.4 16.6 %partial_panel.1 = (f32[2,512,1152]{2,1,0:T(8,128)}, f32[512,128]{1,0:T(8,128)}) custom-call(f32[1152,512]{1,0:T(8,128)S(1)} %bitcast.4, f32[1152,2304]{1,0:T(8,128)} %r_ref.3, f32[1152,128]{1,0:T(8,128)S(1)} %copy-done), custom_call_target="tpu_custom_call" | custom-call | tf_op jit(solution)/shard_map/partial_panel/pallas_call | solution.py:192
  50.0 0.0 all-reduce.2.cloned.1.call-update
  50.0 0.0 copy-start.7
  50.0 0.0 copy-start.1
  50.0 103.0 %panels.1 = (f32[2,8,64,1152]{3,2,1,0:T(8,128)}, f32[8,64,1152]{2,1,0:T(8,128)S(1)}, f32[2,8,32,512]{3,2,1,0:T(8,128)S(1)}) custom-call(f32[2,8,64,1152]{3,2,1,0:T(8,128)} %bitcast.8, f32[1152,512]{1,0:T(8,128)S(1)} %bitcast.5), custom_call_target="tpu_custom_call" | custom-call | tf_op jit(solution)/shard_map/panels/pallas_call | solution.py:345
  153.0 0.0 copy-start.2
  153.0 1.4 copy-done.2
  154.4 0.0 copy-start.4
  154.4 1.0 copy-done.4
  155.4 0.0 copy-start.3
  155.4 1.7 copy-done.3
  157.1 0.0 copy-start.5
  157.1 1.2 copy-done.5
  158.3 19.8 %gain.1 = (bf16[1152,512]{1,0:T(8,128)(2,1)S(1)}, bf16[1152,512]{1,0:T(8,128)(2,1)S(1)}) custom-call(f32[2,8,32,512]{3,2,1,0:T(8,128)S(1)} %copy-done.5, f32[512,1152]{1,0:T(8,128)S(1)} %bitcast.6), custom_call_target="tpu_custom_call" | custom-call | tf_op jit(solution)/shard_map/gain/pallas_call | solution.py:407
  178.1 21.4 %all-reduce.2.cloned.1.call-done = f32[512,128]{1,0:T(8,128)} async-done(((f32[512,128]{1,0:T(8,128)}), f32[512,128]{1,0:T(8,128)}) %all-reduce.2.cloned.1.call-update) | async-done | bytes 262160 | tf_op jit(solution)/shard_map/psum | solution.py:457
  199.5 0.0 copy-done.7
  199.5 1.1 convert_subtract_fusion.resid_ref
  200.6 0.0 copy-done.1
  200.6 17.5 %update.1 = (f32[1152,2304]{1,0:T(8,128)}, f32[1152,128]{1,0:T(8,128)}) custom-call(bf16[1152,512]{1,0:T(8,128)(2,1)S(1)} %get-tuple-element.12.mh_ref, bf16[1152,512]{1,0:T(8,128)(2,1)S(1)} %get-tuple-element.13.ml_ref, f32[2,512,1152]{2,1,0:T(8,128)} %bitcast.7, f32[1152,2304]{1,0:T(8,128)} %r_ref.3, f32[512,128]{1,0:T(8,128)S(1)} %convert_subtract_fusion.resid_ref, ...), custom_call_target="tpu_custom_call" | custom-call | tf_op jit(solution)/shard_map/update/pallas_call | solution.py:433
  (1 shorter events, 0.0 us)
Async XLA Ops:
  7.2 192.3 %all-reduce.2.cloned.1.call-start = ((), (), s32[]{:S(2)}) async-start(), calls=%async_computation | async-start | bytes 524288 | tf_op jit(solution)/shard_map/psum | solution.py:457
  7.2 1.0 copy-start.6
  32.3 1.1 copy-start
  50.0 149.5 %copy-start.7 = (s32[512]{0:T(512)S(1)}, s32[512]{0:T(512)}, u32[]{:S(2)}) copy-start(s32[512]{0:T(512)} %param.5) | copy-start | bytes 6148
  50.0 150.6 %copy-start.1 = (f32[1152,128]{1,0:T(8,128)S(1)}, f32[1152,128]{1,0:T(8,128)}, u32[]{:S(2)}) copy-start(f32[1152,128]{1,0:T(8,128)} %w_ref.3) | copy-start | bytes 1769476
  153.0 1.4 copy-start.2
  154.4 1.0 copy-start.4
  155.4 1.7 copy-start.3
  157.1 1.2 copy-start.5
Sparse Core Ops, SparseCore 0:
  50.1 149.3 all-reduce.1

commit v2 on v1

v2 whole, which is shorter than its diff:
```python
import jax
import jax.numpy as jnp
from jax import lax
from jax.experimental import pallas as pl
from jax.experimental.pallas import tpu as pltpu
from jax.sharding import PartitionSpec as P

F32 = jnp.float32
BF16 = jnp.bfloat16
MESH = pl.DeviceIdType.MESH
ALL = 512
CHUNK = 64
MIB = 1 << 20
VMEM_PANELS = 48 * MIB
VMEM_UPDATE = 48 * MIB


def split(value):
    hi = value.astype(BF16)
    lo = (value - hi.astype(F32)).astype(BF16)
    return hi, lo


def mm(left, right):
    return jnp.dot(left, right, preferred_element_type=F32)


def dot3(left, right):
    (lh, ll), (rh, rl) = left, right
    return mm(lh, rh) + (mm(lh, rl) + mm(ll, rh))


class Place:
    def __init__(self):
        self.row, self.col = row, col = lax.axis_index("row"), lax.axis_index("col")
        self.core = core = lax.rem(row, 2)
        self.chip_row = chip_row = row // 2
        self.y_hi, self.x = y_hi, x = chip_row // 4, lax.rem(chip_row, 4)
        self.y_lo, self.z = y_lo, z = col // 4, lax.rem(col, 4)
        self.sibling = (chip_row * 2 + (1 - core), col)
        self.x_up = ((y_hi * 4 + lax.rem(x + 1, 4)) * 2 + core, col)
        self.x_down = ((y_hi * 4 + lax.rem(x + 3, 4)) * 2 + core, col)
        self.x_far = ((y_hi * 4 + lax.rem(x + 2, 4)) * 2 + core, col)
        self.y_far = (((1 - y_hi) * 4 + x) * 2 + core, col)
        self.z_up = (row, y_lo * 4 + lax.rem(z + 1, 4))
        self.z_down = (row, y_lo * 4 + lax.rem(z + 3, 4))
        self.y_near = (row, (1 - y_lo) * 4 + z)
        self.y_next = (((1 - y_hi) * 4 + x) * 2 + core, (1 - y_lo) * 4 + z)
        self.swapped = ((y_hi * 4 + z) * 2 + core, y_lo * 4 + x)
        self.inner = y_hi != y_lo
        self.off_diagonal = x != z


class Copies:
    def __init__(self, send_sems, recv_sems):
        self.send_sems, self.recv_sems = send_sems, recv_sems
        self.count = 0
        self.started = []

    def take(self):
        self.count += 1
        return self.count - 1

    def make(self, index, src, dst, device):
        return pltpu.make_async_remote_copy(
            src_ref=src, dst_ref=dst, send_sem=self.send_sems.at[index], recv_sem=self.recv_sems.at[index],
            device_id=device, device_id_type=MESH)

    def start(self, src, dst, device):
        index = self.take()
        copy = self.make(index, src, dst, device)
        copy.start()
        self.started.append(copy)
        return index

    def arrived(self, index, landing, device):
        self.make(index, landing, landing, device).wait_recv()

    def finish(self):
        for copy in self.started:
            copy.wait_send()


def greet(devices, maybe):
    barrier = pltpu.get_barrier_semaphore()
    total = jnp.int32(len(devices))
    for device in devices:
        pl.semaphore_signal(barrier, inc=1, device_id=device, device_id_type=MESH)
    for there, device in maybe:
        total = total + jnp.where(there, 1, 0)

        @pl.when(there)
        def _():
            pl.semaphore_signal(barrier, inc=1, device_id=device, device_id_type=MESH)

    pl.semaphore_wait(barrier, total)


class Gather:
    def __init__(self, copies, buf, pair_at, ring_at, pair, up, down, rows):
        self.c, self.buf, self.rows = copies, buf, rows
        self.a, self.b = pair_at, ring_at
        self.pair, self.up, self.down = pair, up, down

    def slot(self, pair_step, ring_step):
        a = self.a if pair_step == 0 else 1 - self.a
        return a * 4 + lax.rem(self.b + ring_step, 4)

    def part(self, pair_step, ring_step, half=None):
        at = self.slot(pair_step, ring_step)
        if half is None:
            return self.buf.at[at]
        n = self.rows // 2
        return self.buf.at[at, pl.ds(half * n, n)]

    def same(self, part, device):
        return self.c.start(part, part, device)

    def own(self):
        mine = self.part(0, 0)
        self.i_up = self.same(mine, self.up)
        self.i_down = self.same(mine, self.down)
        self.i_pair = self.same(mine, self.pair)

    def forward_own(self):
        self.c.arrived(self.i_up, self.part(0, 3), self.down)
        self.h_up = self.same(self.part(0, 3, 0), self.up)
        self.c.arrived(self.i_down, self.part(0, 1), self.up)
        self.h_down = self.same(self.part(0, 1, 1), self.down)

    def pair_across(self):
        self.c.arrived(self.i_pair, self.part(1, 0), self.pair)
        self.q_up = self.same(self.part(1, 0), self.up)
        self.q_down = self.same(self.part(1, 0), self.down)

    def far_own(self):
        self.c.arrived(self.h_up, self.part(0, 2, 0), self.down)
        self.c.arrived(self.h_down, self.part(0, 2, 1), self.up)

    def far_by_pair(self):
        self.f_pair = self.same(self.part(0, 2), self.pair)

    def end_by_pair(self):
        self.c.arrived(self.q_up, self.part(1, 3), self.down)
        self.c.arrived(self.q_down, self.part(1, 1), self.up)
        self.c.arrived(self.f_pair, self.part(1, 2), self.pair)

    def forward_pair(self):
        self.c.arrived(self.q_up, self.part(1, 3), self.down)
        self.g_up = self.same(self.part(1, 3, 0), self.up)
        self.c.arrived(self.q_down, self.part(1, 1), self.up)
        self.g_down = self.same(self.part(1, 1, 1), self.down)

    def end_by_ring(self):
        self.c.arrived(self.g_up, self.part(1, 2, 0), self.down)
        self.c.arrived(self.g_down, self.part(1, 2, 1), self.up)


def stack_left(ref, value):
    hi, lo = split(value)
    depth = value.shape[1]
    ref[:, 0:depth] = hi
    ref[:, depth:2 * depth] = hi
    ref[:, 2 * depth:] = lo


def stack_right(value):
    hi, lo = split(value)
    return jnp.concatenate([hi, lo, hi], 0)


def eye_of(order):
    rows = lax.broadcasted_iota(jnp.int32, (order, order), 0)
    cols = lax.broadcasted_iota(jnp.int32, (order, order), 1)
    return jnp.where(rows == cols, 1.0, 0.0).astype(F32)


BLOCKS = 3
BLOCK = 384


def panels_kernel(x_ref, w_ref, r_ref, uc_ref, ur_ref, a_ref, g_ref, fit_ref,
                  rv, xr, xs, part, from_sib, acc, ra, rb, ry, relay, s_all, sp, rs0, sh, rs1, sh2, rs2,
                  fx, rf0, fh, rf1, fh2, rf2, local_sems, send_sems, recv_sems):
    at = Place()
    k, p, col = at.core, at.chip_row, at.col
    rows = x_ref.shape[0]
    turns = [(1 - k, j) for j in range(BLOCKS)] + [(k, j) for j in range(BLOCKS)]

    def columns(h, j):
        return pl.ds(pl.multiple_of((h * BLOCKS + j) * BLOCK, 128), BLOCK)

    loads = []
    for i, (h, j) in enumerate(turns):
        loads.append(pltpu.make_async_copy(r_ref.at[:, columns(h, j)], rv.at[i], local_sems.at[i]))
        loads[-1].start()
    xr[col] = x_ref[...]
    greet([at.sibling, at.x_up, at.x_down, at.x_far, at.y_far, at.z_up, at.z_down, at.y_near],
          [(at.inner, at.y_next), (at.off_diagonal, at.swapped)])
    copies = Copies(send_sems, recv_sems)

    gx = Gather(copies, xr, at.y_lo, at.z, at.y_near, at.z_up, at.z_down, rows)
    gx.own()
    gx.forward_own()
    gx.pair_across()
    gx.far_own()
    gx.far_by_pair()
    gx.end_by_pair()
    stack_left(xs, xr[...].reshape(8 * rows, ALL).T)

    fx[...] = mm(xs[...], stack_right(w_ref[...]))
    n = ALL // 2
    f0 = copies.start(fx.at[pl.ds(pl.multiple_of((1 - k) * n, n), n)], rf0, at.sibling)

    def product(i):
        h, j = turns[i]
        loads[i].wait()
        value = mm(xs[...], stack_right(rv[i]))
        part[h, :, :, j * BLOCK:(j + 1) * BLOCK] = value.reshape(8, CHUNK, BLOCK)

    sib = []
    for j in range(BLOCKS):
        product(j)
        piece = (slice(None), slice(None), slice(j * BLOCK, (j + 1) * BLOCK))
        sib.append(copies.start(part.at[(1 - k,) + piece], from_sib.at[piece], at.sibling))
        if j == 0:
            copies.arrived(f0, rf0, at.sibling)
            fh[...] = fx[pl.ds(pl.multiple_of(k * n, n), n)] + rf0[...]
            f1 = [copies.start(fh, rf1.at[i], d) for i, d in enumerate((at.x_up, at.x_down, at.x_far))]
    for i, d in enumerate((at.x_down, at.x_up, at.x_far)):
        copies.arrived(f1[i], rf1.at[i], d)
    fh2[...] = (fh[...] + rf1[2]) + (rf1[0] + rf1[1])
    f2 = copies.start(fh2, rf2, at.y_far)
    for j in range(BLOCKS):
        product(BLOCKS + j)
    copies.arrived(f2, rf2, at.y_far)
    mine_fit = fit_ref.at[pl.ds(pl.multiple_of(k * n, n), n)]
    mine_fit[...] = fh2[...] + rf2[...]
    f3 = copies.start(mine_fit, mine_fit, at.sibling)
    for j in range(BLOCKS):
        copies.arrived(sib[j], from_sib.at[:, :, j * BLOCK:(j + 1) * BLOCK], at.sibling)

    def chunk(y_step, x_step):
        y = at.y_hi if y_step == 0 else 1 - at.y_hi
        return y * 4 + lax.rem(at.x + x_step, 4)

    def add_sibling(y, x_step):
        ch = chunk(y, x_step)
        acc[ch] = part[k, ch] + from_sib[ch]
        return ch

    half = CHUNK // 2
    low, high = pl.ds(0, half), pl.ds(half, half)
    a_up, a_down, b_up, b_down = {}, {}, {}, {}
    for y in (1, 0):
        ch = add_sibling(y, 2)
        a_up[y] = copies.start(acc.at[ch, low], ra.at[0, y], at.x_up)
        a_down[y] = copies.start(acc.at[ch, high], ra.at[1, y], at.x_down)
    for y in (1, 0):
        for x_step in (1, 3, 0):
            add_sibling(y, x_step)
    for y in (1, 0):
        ch = chunk(y, 1)
        copies.arrived(a_up[y], ra.at[0, y], at.x_down)
        acc[ch, low] = acc[ch, low] + ra[0, y]
        b_up[y] = copies.start(acc.at[ch], rb.at[0, y], at.x_up)
        ch = chunk(y, 3)
        copies.arrived(a_down[y], ra.at[1, y], at.x_up)
        acc[ch, high] = acc[ch, high] + ra[1, y]
        b_down[y] = copies.start(acc.at[ch], rb.at[1, y], at.x_down)

    def add_x(y):
        ch = chunk(y, 0)
        copies.arrived(b_up[y], rb.at[0, y], at.x_down)
        copies.arrived(b_down[y], rb.at[1, y], at.x_up)
        return acc[ch] + (rb[0, y] + rb[1, y])

    ch = chunk(1, 0)
    acc[ch] = add_x(1)
    c_far = copies.start(acc.at[ch], ry, at.y_far)
    mine = add_x(0)
    copies.arrived(c_far, ry, at.y_far)
    mine = mine + ry[...]
    uc_ref[k, p] = mine

    own_block = uc_ref.at[k]
    t0 = copies.take()
    step_y = copies.make(t0, uc_ref.at[k, p], relay, at.y_next)

    @pl.when(at.inner)
    def _():
        step_y.start()

    gc = Gather(copies, own_block, at.y_hi, at.x, at.y_far, at.x_up, at.x_down, CHUNK)
    gr = Gather(copies, ur_ref, at.y_lo, at.z, at.y_near, at.z_up, at.z_down, CHUNK)

    def to_sibling(pair_step, ring_step):
        piece = gc.part(pair_step, ring_step)
        return copies.start(piece, piece, at.sibling)

    gc.own()
    u = {(0, 0): to_sibling(0, 0)}

    @pl.when(at.inner)
    def _():
        copies.make(t0, relay, relay, at.y_next).wait_recv()
        step_y.wait_send()

    @pl.when(jnp.logical_not(at.inner))
    def _():
        relay[...] = uc_ref[k, p]

    t1 = copies.take()
    step_xz = copies.make(t1, relay, ur_ref.at[at.y_lo * 4 + at.x], at.swapped)

    @pl.when(at.off_diagonal)
    def _():
        step_xz.start()

    gc.forward_own()
    u[(0, 3)] = to_sibling(0, 3)
    u[(0, 1)] = to_sibling(0, 1)

    @pl.when(at.off_diagonal)
    def _():
        copies.make(t1, ur_ref.at[col], ur_ref.at[col], at.swapped).wait_recv()
        step_xz.wait_send()

    @pl.when(jnp.logical_not(at.off_diagonal))
    def _():
        ur_ref[col] = relay[...]

    gr.own()

    sp[...] = dot3(split(ur_ref[col]), split(xr[...].reshape(8 * rows, ALL)))
    s0 = copies.start(sp.at[pl.ds(pl.multiple_of((1 - k) * half, half), half)], rs0, at.sibling)
    gc.pair_across()
    u[(1, 0)] = to_sibling(1, 0)
    copies.arrived(s0, rs0, at.sibling)
    sh[...] = sp[pl.ds(pl.multiple_of(k * half, half), half)] + rs0[...]
    s1 = [copies.start(sh, rs1.at[i], d) for i, d in enumerate((at.x_up, at.x_down, at.x_far))]
    gr.forward_own()
    gr.pair_across()
    for i, d in enumerate((at.x_down, at.x_up, at.x_far)):
        copies.arrived(s1[i], rs1.at[i], d)
    sh2[...] = (sh[...] + rs1[2]) + (rs1[0] + rs1[1])
    s2 = copies.start(sh2, rs2, at.y_far)
    copies.arrived(s2, rs2, at.y_far)
    s_all[k, col] = sh2[...] + rs2[...]
    gs = Gather(copies, s_all.at[k], at.y_lo, at.z, at.y_near, at.z_up, at.z_down, half)
    gs.own()
    gc.far_own()
    u[(0, 2)] = to_sibling(0, 2)
    gc.forward_pair()
    u[(1, 3)] = to_sibling(1, 3)
    u[(1, 1)] = to_sibling(1, 1)
    gs.forward_own()
    gs.pair_across()
    gs.far_own()
    gs.forward_pair()
    gs.end_by_ring()
    s4 = copies.start(s_all.at[k], s_all.at[k], at.sibling)
    gr.far_own()
    gr.forward_pair()
    gc.end_by_ring()
    u[(1, 2)] = to_sibling(1, 2)
    copies.arrived(s4, s_all.at[1 - k], at.sibling)

    for c in range(8):
        for h in range(2):
            a_ref[pl.ds(c * CHUNK + h * half, half)] = s_all[h, c]
    eye = eye_of(ALL)
    a_ref[...] = a_ref[...] + eye
    bound = jnp.max(jnp.sum(jnp.abs(a_ref[...]), axis=0, keepdims=True))
    scale = 2.0 / (1.0 + bound)
    g_ref[...] = scale * (2.0 * eye - scale * a_ref[...])

    @pl.loop(0, 3)
    def _(_):
        g = split(g_ref[...])
        error = eye_of(ALL) - dot3(split(a_ref[...]), g)
        g_ref[...] = g_ref[...] + dot3(g, split(error))

    gr.end_by_ring()
    other = uc_ref.at[1 - k]
    for (pair_step, ring_step), index in u.items():
        copies.arrived(index, other.at[gc.slot(pair_step, ring_step)], at.sibling)
    copies.arrived(f3, fit_ref.at[pl.ds(pl.multiple_of((1 - k) * n, n), n)], at.sibling)
    copies.finish()


def panels(features_t, head, tile):
    rows, examples = features_t.shape
    depth, width = tile.shape[0], tile.shape[1] // 2
    classes = head.shape[1]
    half = CHUNK // 2
    vmem = pl.BlockSpec(memory_space=pltpu.VMEM)
    dma = pltpu.SemaphoreType.DMA
    return pl.pallas_call(
        panels_kernel,
        out_shape=(
            jax.ShapeDtypeStruct((2, 8, CHUNK, width), F32),
            jax.ShapeDtypeStruct((8, CHUNK, width), F32),
            jax.ShapeDtypeStruct((ALL, ALL), F32),
            jax.ShapeDtypeStruct((ALL, ALL), F32),
            jax.ShapeDtypeStruct((ALL, classes), F32),
        ),
        in_specs=[vmem, vmem, pl.BlockSpec(memory_space=pl.ANY)],
        out_specs=(vmem,) * 5,
        scratch_shapes=[
            pltpu.VMEM((2 * BLOCKS, depth, BLOCK), F32),
            pltpu.VMEM((8, rows, examples), F32),
            pltpu.VMEM((examples, 3 * depth), BF16),
            pltpu.VMEM((2, 8, CHUNK, width), F32),
            pltpu.VMEM((8, CHUNK, width), F32),
            pltpu.VMEM((8, CHUNK, width), F32),
            pltpu.VMEM((2, 2, half, width), F32),
            pltpu.VMEM((2, 2, CHUNK, width), F32),
            pltpu.VMEM((CHUNK, width), F32),
            pltpu.VMEM((CHUNK, width), F32),
            pltpu.VMEM((2, 8, half, ALL), F32),
            pltpu.VMEM((CHUNK, ALL), F32),
            pltpu.VMEM((half, ALL), F32),
            pltpu.VMEM((half, ALL), F32),
            pltpu.VMEM((3, half, ALL), F32),
            pltpu.VMEM((half, ALL), F32),
            pltpu.VMEM((half, ALL), F32),
            pltpu.VMEM((ALL, classes), F32),
            pltpu.VMEM((ALL // 2, classes), F32),
            pltpu.VMEM((ALL // 2, classes), F32),
            pltpu.VMEM((3, ALL // 2, classes), F32),
            pltpu.VMEM((ALL // 2, classes), F32),
            pltpu.VMEM((ALL // 2, classes), F32),
            dma((2 * BLOCKS,)),
            dma((80,)),
            dma((80,)),
        ],
        compiler_params=pltpu.CompilerParams(collective_id=0, has_side_effects=True, vmem_limit_bytes=VMEM_PANELS),
        name="panels",
    )(features_t, head, tile)


def update_kernel(a_ref, g_ref, ur_ref, u_ref, r_ref, targets_ref, fit_ref, w_ref, out_ref, head_ref, inv_ref, gain_ref):
    at = pl.program_id(0)

    @pl.when(at == 0)
    def _():
        inv_ref[...] = g_ref[...]

        def more(state):
            step, size = state
            return (step < 60) & (size > 1e-7)

        def refine(state):
            step, _ = state
            g = inv_ref[...]
            error = eye_of(ALL) - jnp.dot(a_ref[...], g, precision=lax.Precision.HIGHEST, preferred_element_type=F32)
            inv_ref[...] = g + dot3(split(g), split(error))
            return step + 1, jnp.sum(error * error)

        lax.while_loop(more, refine, (jnp.int32(0), F32(1.0)))
        stack_left(gain_ref, dot3(split(ur_ref[...].T), split(inv_ref[...])))
        head_ref[...] = w_ref[...] + mm(gain_ref[...], stack_right(targets_ref[...] - fit_ref[...]))

    block = r_ref[:, pl.ds(pl.multiple_of(at * BLOCK, 128), BLOCK)]
    out_ref[...] = block - mm(gain_ref[...], stack_right(u_ref[0]))


def update(inv_system, inverse, rows_t, cols_t, tile, targets, fitted, head):
    rows = tile.shape[0]
    vmem = pl.BlockSpec(memory_space=pltpu.VMEM)
    return pl.pallas_call(
        update_kernel,
        grid=(2 * BLOCKS,),
        out_shape=(jax.ShapeDtypeStruct(tile.shape, F32), jax.ShapeDtypeStruct(head.shape, F32)),
        in_specs=[
            vmem,
            vmem,
            vmem,
            pl.BlockSpec((1, ALL, BLOCK), lambda i: (i // BLOCKS, 0, lax.rem(i, BLOCKS))),
            vmem,
            vmem,
            vmem,
            vmem,
        ],
        out_specs=(pl.BlockSpec((rows, BLOCK), lambda i: (0, i)), pl.BlockSpec(head.shape, lambda i: (0, 0))),
        scratch_shapes=[pltpu.VMEM((ALL, ALL), F32), pltpu.VMEM((rows, 3 * ALL), BF16)],
        compiler_params=pltpu.CompilerParams(vmem_limit_bytes=VMEM_UPDATE),
        name="update",
    )(inv_system, inverse, rows_t, cols_t, tile, targets, fitted, head)


def on_device(features_t, labels, inv_corr, heads):
    width = heads.shape[1]
    classes = lax.axis_index("col") * width + jnp.arange(width, dtype=jnp.int32)
    targets = (labels[:, None] == classes[None, :]).astype(F32)
    cols_t, rows_t, system, inverse, fitted = panels(features_t, heads, inv_corr)
    block = cols_t.shape[3]
    return update(system, inverse, rows_t.reshape(ALL, block), cols_t.reshape(2, ALL, block), inv_corr, targets, fitted, heads)


def solution(mesh):
    placed = (P(("row", "col"), None), P(), P("row", "col"), P("row", "col"))
    return jax.shard_map(
        on_device,
        mesh=mesh,
        in_specs=placed,
        out_specs=(P("row", "col"), P("row", "col")),
        check_vma=False,
    )
```

time: 226 us -> 166 us (0.73)
  Pallas kernels: 181 us -> 159 us
  waiting for transfers between devices: 21.4 us -> 0 us
  between operations: 14.1 us -> 0.67 us
  local copies, waits for them, and re-layouts: 7.31 us -> 2.02 us
    pallas_call x4 -> x1, Pallas kernels: 78 us -> 29.6 us  [update(): pl.pallas_call(update_kernel, grid=(2 * BLOCKS,), out_shape=(jax.ShapeDty...]
    pallas_call x1, Pallas kernels: 103 us -> 130 us  [panels(): pl.pallas_call(panels_kernel, out_shape=(jax.ShapeDtypeStruct((2, 8, CHUN...]
    psum x1 -> x0, waiting for transfers between devices: 21.4 us -> none  [on_device(): resid = targets - lax.psum(fitted, 'row')]
    unnamed x16 -> x4, local copies, waits for them, and re-layouts: 7.31 us -> 2.02 us
  transfers between devices with their start and end apart: 1 -> 0, of which waited for: 1 -> 0; matrix products, arithmetic and copies ran while one was open for 0% -> 0% of each run, Pallas kernels for 55% -> 0%
where the time goes in v2:
time: 166 us; the launch traced here: 163 us
  Pallas kernels  159 us (96%)
  local copies, waits for them, and re-layouts  2.02 us (1%)
    pallas_call x1, Pallas kernels, panels(): pl.pallas_call(panels_kernel, out_shape=(jax.ShapeDtypeStruct((2, 8, CHUN...  130 us
    pallas_call x1, Pallas kernels, update(): pl.pallas_call(update_kernel, grid=(2 * BLOCKS,), out_shape=(jax.ShapeDty...  29.6 us

profile of v2, /device:TPU:0, one launch (start us, length us, event | category | flops | bytes accessed | tf_op | source)
XLA Modules:
  0.0 162.9 jit_solution(436428274425428852)
XLA Ops:
  0.6 0.8 compare_convert_fusion.targets_ref
  1.5 0.0 copy-start
  1.5 1.1 copy-done
  2.5 0.0 copy-start.1
  2.5 1.0 copy-done.1
  3.5 129.8 %panels.1 = (f32[2,8,64,1152]{3,2,1,0:T(8,128)}, f32[8,64,1152]{2,1,0:T(8,128)S(1)}, f32[512,512]{1,0:T(8,128)S(1)}, f32[512,512]{1,0:T(8,128)S(1)}, f32[512,128]{1,0:T(8,128)S(1)}) custom-call(f32[144,512]{1,0:T(8,128)S(1)} %copy-done.1, f32[1152,128]{1,0:T(8,128)S(1)} %copy-done, f32[1152,2304]{1,0:T(8,128)} %r_ref.3), custom_call_target="tpu_custom_call" | custom-call | tf_op jit(solution)/shard_map/panels/pallas_call | solution.py:399
  133.3 29.6 %update.1 = (f32[1152,2304]{1,0:T(8,128)}, f32[1152,128]{1,0:T(8,128)}) custom-call(f32[512,512]{1,0:T(8,128)S(1)} %get-tuple-element.7.a_ref, f32[512,512]{1,0:T(8,128)S(1)} %get-tuple-element.8.g_ref, f32[512,1152]{1,0:T(8,128)S(1)} %bitcast.2, f32[2,512,1152]{2,1,0:T(8,128)} %bitcast.3, f32[1152,2304]{1,0:T(8,128)} %r_ref.3, ...), custom_call_target="tpu_custom_call" | custom-call | tf_op jit(solution)/shard_map/update/pallas_call | solution.py:472
  (1 shorter events, 0.0 us)
Async XLA Ops:
  1.5 1.1 copy-start
  2.5 1.0 copy-start.1

commit v3 on v2

--- a/solution.py
+++ b/solution.py
@@ -49,6 +49,12 @@
         self.swapped = ((y_hi * 4 + z) * 2 + core, y_lo * 4 + x)
         self.inner = y_hi != y_lo
         self.off_diagonal = x != z
+        between = lax.rem(y_hi + y_lo, 2)
+        far_y, near_y = lax.rem(y_hi + between, 2), lax.rem(y_lo + 1 - between, 2)
+        self.sum_to = ((far_y * 4 + x) * 2 + core, near_y * 4 + z)
+        back_y, side_y = lax.rem(y_hi + 1 - between, 2), lax.rem(y_lo + between, 2)
+        self.spread_to = ((back_y * 4 + x) * 2 + core, side_y * 4 + z)
+        self.spread_slot = far_y * 4 + x
 
 
 class Copies:
@@ -117,10 +123,13 @@
         return self.c.start(part, part, device)
 
     def own(self):
+        self.own_ring()
+        self.i_pair = self.same(self.part(0, 0), self.pair)
+
+    def own_ring(self):
         mine = self.part(0, 0)
         self.i_up = self.same(mine, self.up)
         self.i_down = self.same(mine, self.down)
-        self.i_pair = self.same(mine, self.pair)
 
     def forward_own(self):
         self.c.arrived(self.i_up, self.part(0, 3), self.down)
@@ -179,8 +188,8 @@
 BLOCK = 384
 
 
-def panels_kernel(x_ref, w_ref, r_ref, uc_ref, ur_ref, a_ref, g_ref, fit_ref,
-                  rv, xr, xs, part, from_sib, acc, ra, rb, ry, relay, s_all, sp, rs0, sh, rs1, sh2, rs2,
+def panels_kernel(x_ref, w_ref, r_ref, uc_ref, ur_ref, a_ref, g_ref, size_ref, fit_ref,
+                  wv, rv, xr, xs, part, from_sib, acc, ra, rb, ry, ry2, relay, s_all, sp, rs0, sh, rs1, sh2, rs2,
                   fx, rf0, fh, rf1, fh2, rf2, local_sems, send_sems, recv_sems):
     at = Place()
     k, p, col = at.core, at.chip_row, at.col
@@ -190,13 +199,17 @@
     def columns(h, j):
         return pl.ds(pl.multiple_of((h * BLOCKS + j) * BLOCK, 128), BLOCK)
 
+    own_x = pltpu.make_async_copy(x_ref, xr.at[col], local_sems.at[2 * BLOCKS])
+    own_x.start()
+    own_w = pltpu.make_async_copy(w_ref, wv, local_sems.at[2 * BLOCKS + 1])
+    own_w.start()
     loads = []
     for i, (h, j) in enumerate(turns):
         loads.append(pltpu.make_async_copy(r_ref.at[:, columns(h, j)], rv.at[i], local_sems.at[i]))
         loads[-1].start()
-    xr[col] = x_ref[...]
     greet([at.sibling, at.x_up, at.x_down, at.x_far, at.y_far, at.z_up, at.z_down, at.y_near],
           [(at.inner, at.y_next), (at.off_diagonal, at.swapped)])
+    own_x.wait()
     copies = Copies(send_sems, recv_sems)
 
     gx = Gather(copies, xr, at.y_lo, at.z, at.y_near, at.z_up, at.z_down, rows)
@@ -208,7 +221,8 @@
     gx.end_by_pair()
     stack_left(xs, xr[...].reshape(8 * rows, ALL).T)
 
-    fx[...] = mm(xs[...], stack_right(w_ref[...]))
+    own_w.wait()
+    fx[...] = mm(xs[...], stack_right(wv[...]))
     n = ALL // 2
     f0 = copies.start(fx.at[pl.ds(pl.multiple_of((1 - k) * n, n), n)], rf0, at.sibling)
 
@@ -227,16 +241,8 @@
             copies.arrived(f0, rf0, at.sibling)
             fh[...] = fx[pl.ds(pl.multiple_of(k * n, n), n)] + rf0[...]
             f1 = [copies.start(fh, rf1.at[i], d) for i, d in enumerate((at.x_up, at.x_down, at.x_far))]
-    for i, d in enumerate((at.x_down, at.x_up, at.x_far)):
-        copies.arrived(f1[i], rf1.at[i], d)
-    fh2[...] = (fh[...] + rf1[2]) + (rf1[0] + rf1[1])
-    f2 = copies.start(fh2, rf2, at.y_far)
     for j in range(BLOCKS):
         product(BLOCKS + j)
-    copies.arrived(f2, rf2, at.y_far)
-    mine_fit = fit_ref.at[pl.ds(pl.multiple_of(k * n, n), n)]
-    mine_fit[...] = fh2[...] + rf2[...]
-    f3 = copies.start(mine_fit, mine_fit, at.sibling)
     for j in range(BLOCKS):
         copies.arrived(sib[j], from_sib.at[:, :, j * BLOCK:(j + 1) * BLOCK], at.sibling)
 
@@ -259,6 +265,10 @@
     for y in (1, 0):
         for x_step in (1, 3, 0):
             add_sibling(y, x_step)
+    for i, d in enumerate((at.x_down, at.x_up, at.x_far)):
+        copies.arrived(f1[i], rf1.at[i], d)
+    fh2[...] = (fh[...] + rf1[2]) + (rf1[0] + rf1[1])
+    f2 = copies.start(fh2, rf2, at.y_far)
     for y in (1, 0):
         ch = chunk(y, 1)
         copies.arrived(a_up[y], ra.at[0, y], at.x_down)
@@ -275,51 +285,66 @@
         copies.arrived(b_down[y], rb.at[1, y], at.x_up)
         return acc[ch] + (rb[0, y] + rb[1, y])
 
-    ch = chunk(1, 0)
-    acc[ch] = add_x(1)
-    c_far = copies.start(acc.at[ch], ry, at.y_far)
-    mine = add_x(0)
-    copies.arrived(c_far, ry, at.y_far)
-    mine = mine + ry[...]
-    uc_ref[k, p] = mine
+    other, own = chunk(1, 0), chunk(0, 0)
+    acc[other] = add_x(1)
+    c1 = copies.start(acc.at[other], ry, at.sum_to)
+    acc[own] = add_x(0)
+    c2 = copies.take()
+    inner_sum = copies.make(c2, acc.at[own], ry2, at.y_next)
+
+    @pl.when(at.inner)
+    def _():
+        inner_sum.start()
+
+    copies.arrived(c1, ry, at.sum_to)
+
+    @pl.when(at.inner)
+    def _():
+        copies.make(c2, ry2, ry2, at.y_next).wait_recv()
+        relay[...] = ry[...] + ry2[...]
+        inner_sum.wait_send()
+
+    @pl.when(jnp.logical_not(at.inner))
+    def _():
+        relay[...] = acc[own] + ry[...]
+        uc_ref[k, p] = relay[...]
+
+    t1 = copies.take()
+    step_xz = copies.make(t1, relay, ur_ref.at[at.y_lo * 4 + at.x], at.swapped)
+
+    @pl.when(at.off_diagonal)
+    def _():
+        step_xz.start()
+
+    d1 = copies.start(relay, uc_ref.at[k, at.spread_slot], at.spread_to)
+    d2 = copies.take()
+    inner_back = copies.make(d2, relay, uc_ref.at[k, at.spread_slot], at.y_next)
+
+    @pl.when(at.inner)
+    def _():
+        inner_back.start()
 
     own_block = uc_ref.at[k]
-    t0 = copies.take()
-    step_y = copies.make(t0, uc_ref.at[k, p], relay, at.y_next)
-
-    @pl.when(at.inner)
-    def _():
-        step_y.start()
-
     gc = Gather(copies, own_block, at.y_hi, at.x, at.y_far, at.x_up, at.x_down, CHUNK)
     gr = Gather(copies, ur_ref, at.y_lo, at.z, at.y_near, at.z_up, at.z_down, CHUNK)
+    gc.i_pair = d1
 
     def to_sibling(pair_step, ring_step):
         piece = gc.part(pair_step, ring_step)
         return copies.start(piece, piece, at.sibling)
 
-    gc.own()
+    copies.arrived(f2, rf2, at.y_far)
+    mine_fit = fit_ref.at[pl.ds(pl.multiple_of(k * n, n), n)]
+    mine_fit[...] = fh2[...] + rf2[...]
+    f3 = copies.start(mine_fit, mine_fit, at.sibling)
+
+    @pl.when(at.inner)
+    def _():
+        copies.make(d2, uc_ref.at[k, p], uc_ref.at[k, p], at.y_next).wait_recv()
+        inner_back.wait_send()
+
+    gc.own_ring()
     u = {(0, 0): to_sibling(0, 0)}
-
-    @pl.when(at.inner)
-    def _():
-        copies.make(t0, relay, relay, at.y_next).wait_recv()
-        step_y.wait_send()
-
-    @pl.when(jnp.logical_not(at.inner))
-    def _():
-        relay[...] = uc_ref[k, p]
-
-    t1 = copies.take()
-    step_xz = copies.make(t1, relay, ur_ref.at[at.y_lo * 4 + at.x], at.swapped)
-
-    @pl.when(at.off_diagonal)
-    def _():
-        step_xz.start()
-
-    gc.forward_own()
-    u[(0, 3)] = to_sibling(0, 3)
-    u[(0, 1)] = to_sibling(0, 1)
 
     @pl.when(at.off_diagonal)
     def _():
@@ -334,36 +359,34 @@
 
     sp[...] = dot3(split(ur_ref[col]), split(xr[...].reshape(8 * rows, ALL)))
     s0 = copies.start(sp.at[pl.ds(pl.multiple_of((1 - k) * half, half), half)], rs0, at.sibling)
-    gc.pair_across()
-    u[(1, 0)] = to_sibling(1, 0)
     copies.arrived(s0, rs0, at.sibling)
     sh[...] = sp[pl.ds(pl.multiple_of(k * half, half), half)] + rs0[...]
     s1 = [copies.start(sh, rs1.at[i], d) for i, d in enumerate((at.x_up, at.x_down, at.x_far))]
-    gr.forward_own()
-    gr.pair_across()
     for i, d in enumerate((at.x_down, at.x_up, at.x_far)):
         copies.arrived(s1[i], rs1.at[i], d)
     sh2[...] = (sh[...] + rs1[2]) + (rs1[0] + rs1[1])
     s2 = copies.start(sh2, rs2, at.y_far)
+    gc.forward_own()
+    gc.pair_across()
+    for step in ((0, 3), (0, 1), (1, 0)):
+        u[step] = to_sibling(*step)
     copies.arrived(s2, rs2, at.y_far)
     s_all[k, col] = sh2[...] + rs2[...]
     gs = Gather(copies, s_all.at[k], at.y_lo, at.z, at.y_near, at.z_up, at.z_down, half)
     gs.own()
-    gc.far_own()
-    u[(0, 2)] = to_sibling(0, 2)
-    gc.forward_pair()
-    u[(1, 3)] = to_sibling(1, 3)
-    u[(1, 1)] = to_sibling(1, 1)
     gs.forward_own()
     gs.pair_across()
     gs.far_own()
     gs.forward_pair()
     gs.end_by_ring()
     s4 = copies.start(s_all.at[k], s_all.at[k], at.sibling)
-    gr.far_own()
-    gr.forward_pair()
-    gc.end_by_ring()
-    u[(1, 2)] = to_sibling(1, 2)
+    gr.forward_own()
+    gr.pair_across()
+    gc.far_own()
+    u[(0, 2)] = to_sibling(0, 2)
+    gc.forward_pair()
+    for step in ((1, 3), (1, 1)):
+        u[step] = to_sibling(*step)
     copies.arrived(s4, s_all.at[1 - k], at.sibling)
 
     for c in range(8):
@@ -375,16 +398,22 @@
     scale = 2.0 / (1.0 + bound)
     g_ref[...] = scale * (2.0 * eye - scale * a_ref[...])
 
-    @pl.loop(0, 3)
-    def _(_):
+    def refine(_):
         g = split(g_ref[...])
         error = eye_of(ALL) - dot3(split(a_ref[...]), g)
         g_ref[...] = g_ref[...] + dot3(g, split(error))
-
-    gr.end_by_ring()
-    other = uc_ref.at[1 - k]
+        size_ref[...] = jnp.broadcast_to(jnp.sum(error * error), size_ref.shape)
+
+    pl.loop(0, 2)(refine)
+    gr.far_own()
+    gr.far_by_pair()
+    pl.loop(0, 2)(refine)
+    gc.end_by_ring()
+    u[(1, 2)] = to_sibling(1, 2)
+    gr.end_by_pair()
+    other_block = uc_ref.at[1 - k]
     for (pair_step, ring_step), index in u.items():
-        copies.arrived(index, other.at[gc.slot(pair_step, ring_step)], at.sibling)
+        copies.arrived(index, other_block.at[gc.slot(pair_step, ring_step)], at.sibling)
     copies.arrived(f3, fit_ref.at[pl.ds(pl.multiple_of((1 - k) * n, n), n)], at.sibling)
     copies.finish()
 
@@ -403,11 +432,13 @@
             jax.ShapeDtypeStruct((8, CHUNK, width), F32),
             jax.ShapeDtypeStruct((ALL, ALL), F32),
             jax.ShapeDtypeStruct((ALL, ALL), F32),
+            jax.ShapeDtypeStruct((8, 128), F32),
             jax.ShapeDtypeStruct((ALL, classes), F32),
         ),
-        in_specs=[vmem, vmem, pl.BlockSpec(memory_space=pl.ANY)],
-        out_specs=(vmem,) * 5,
+        in_specs=[pl.BlockSpec(memory_space=pltpu.HBM)] * 3,
+        out_specs=(vmem,) * 6,
         scratch_shapes=[
+            pltpu.VMEM(head.shape, F32),
             pltpu.VMEM((2 * BLOCKS, depth, BLOCK), F32),
             pltpu.VMEM((8, rows, examples), F32),
             pltpu.VMEM((examples, 3 * depth), BF16),
@@ -416,6 +447,7 @@
             pltpu.VMEM((8, CHUNK, width), F32),
             pltpu.VMEM((2, 2, half, width), F32),
             pltpu.VMEM((2, 2, CHUNK, width), F32),
+            pltpu.VMEM((CHUNK, width), F32),
             pltpu.VMEM((CHUNK, width), F32),
             pltpu.VMEM((CHUNK, width), F32),
             pltpu.VMEM((2, 8, half, ALL), F32),
@@ -431,7 +463,7 @@
             pltpu.VMEM((3, ALL // 2, classes), F32),
             pltpu.VMEM((ALL // 2, classes), F32),
             pltpu.VMEM((ALL // 2, classes), F32),
-            dma((2 * BLOCKS,)),
+            dma((2 * BLOCKS + 2,)),
             dma((80,)),
             dma((80,)),
         ],
@@ -440,16 +472,22 @@
     )(features_t, head, tile)
 
 
-def update_kernel(a_ref, g_ref, ur_ref, u_ref, r_ref, targets_ref, fit_ref, w_ref, out_ref, head_ref, inv_ref, gain_ref):
+def update_kernel(a_ref, g_ref, size_ref, ur_ref, u_ref, r_ref, labels_ref, fit_ref, w_ref, out_ref, head_ref,
+                  inv_ref, gain_ref, rv, sems):
     at = pl.program_id(0)
 
+    def load(i):
+        return pltpu.make_async_copy(r_ref.at[:, pl.ds(pl.multiple_of(i * BLOCK, 128), BLOCK)], rv.at[i], sems.at[i])
+
     @pl.when(at == 0)
     def _():
+        for i in range(2 * BLOCKS):
+            load(i).start()
         inv_ref[...] = g_ref[...]
 
         def more(state):
             step, size = state
-            return (step < 60) & (size > 1e-7)
+            return (step < 60) & (size > 1e-5)
 
         def refine(state):
             step, _ = state
@@ -458,45 +496,45 @@
             inv_ref[...] = g + dot3(split(g), split(error))
             return step + 1, jnp.sum(error * error)
 
-        lax.while_loop(more, refine, (jnp.int32(0), F32(1.0)))
+        lax.while_loop(more, refine, (jnp.int32(0), size_ref[0, 0]))
         stack_left(gain_ref, dot3(split(ur_ref[...].T), split(inv_ref[...])))
-        head_ref[...] = w_ref[...] + mm(gain_ref[...], stack_right(targets_ref[...] - fit_ref[...]))
-
-    block = r_ref[:, pl.ds(pl.multiple_of(at * BLOCK, 128), BLOCK)]
-    out_ref[...] = block - mm(gain_ref[...], stack_right(u_ref[0]))
-
-
-def update(inv_system, inverse, rows_t, cols_t, tile, targets, fitted, head):
+        width = w_ref.shape[1]
+        classes = lax.axis_index("col") * width + lax.broadcasted_iota(jnp.int32, (width, ALL), 0)
+        targets = jnp.where(labels_ref[...] == classes, 1.0, 0.0).astype(F32).T
+        head_ref[...] = w_ref[...] + mm(gain_ref[...], stack_right(targets - fit_ref[...]))
+
+    load(at).wait()
+    out_ref[...] = rv[at] - mm(gain_ref[...], stack_right(u_ref[0]))
+
+
+def update(system, inverse, size, rows_t, cols_t, tile, labels, fitted, head):
     rows = tile.shape[0]
     vmem = pl.BlockSpec(memory_space=pltpu.VMEM)
     return pl.pallas_call(
         update_kernel,
         grid=(2 * BLOCKS,),
         out_shape=(jax.ShapeDtypeStruct(tile.shape, F32), jax.ShapeDtypeStruct(head.shape, F32)),
-        in_specs=[
-            vmem,
-            vmem,
-            vmem,
+        in_specs=[vmem] * 4 + [
             pl.BlockSpec((1, ALL, BLOCK), lambda i: (i // BLOCKS, 0, lax.rem(i, BLOCKS))),
-            vmem,
-            vmem,
-            vmem,
-            vmem,
+            pl.BlockSpec(memory_space=pl.ANY),
+        ] + [vmem] * 3,
+        out_specs=(pl.BlockSpec((rows, BLOCK), lambda i: (0, i)), pl.BlockSpec(head.shape, lambda i: (0, 0))),
+        scratch_shapes=[
+            pltpu.VMEM((ALL, ALL), F32),
+            pltpu.VMEM((rows, 3 * ALL), BF16),
+            pltpu.VMEM((2 * BLOCKS, rows, BLOCK), F32),
+            pltpu.SemaphoreType.DMA((2 * BLOCKS,)),
         ],
-        out_specs=(pl.BlockSpec((rows, BLOCK), lambda i: (0, i)), pl.BlockSpec(head.shape, lambda i: (0, 0))),
-        scratch_shapes=[pltpu.VMEM((ALL, ALL), F32), pltpu.VMEM((rows, 3 * ALL), BF16)],
         compiler_params=pltpu.CompilerParams(vmem_limit_bytes=VMEM_UPDATE),
         name="update",
-    )(inv_system, inverse, rows_t, cols_t, tile, targets, fitted, head)
+    )(system, inverse, size, rows_t, cols_t, tile, labels.reshape(1, ALL), fitted, head)
 
 
 def on_device(features_t, labels, inv_corr, heads):
-    width = heads.shape[1]
-    classes = lax.axis_index("col") * width + jnp.arange(width, dtype=jnp.int32)
-    targets = (labels[:, None] == classes[None, :]).astype(F32)
-    cols_t, rows_t, system, inverse, fitted = panels(features_t, heads, inv_corr)
+    cols_t, rows_t, system, inverse, size, fitted = panels(features_t, heads, inv_corr)
     block = cols_t.shape[3]
-    return update(system, inverse, rows_t.reshape(ALL, block), cols_t.reshape(2, ALL, block), inv_corr, targets, fitted, heads)
+    return update(system, inverse, size, rows_t.reshape(ALL, block), cols_t.reshape(2, ALL, block), inv_corr, labels,
+                  fitted, heads)
 
 
 def solution(mesh):

time: 166 us -> 157 us (0.946)
  Pallas kernels: 159 us -> 153 us
    pallas_call x1, Pallas kernels: 29.6 us -> 20.6 us  [update(): pl.pallas_call(update_kernel, grid=(2 * BLOCKS,), out_shape=(jax.ShapeDty...]
    pallas_call x1, Pallas kernels: 130 us -> 132 us  [panels(): pl.pallas_call(panels_kernel, out_shape=(jax.ShapeDtypeStruct((2, 8, CHUN...]
where the time goes in v3:
time: 157 us; the launch traced here: 156 us
  Pallas kernels  153 us (97%)
  local copies, waits for them, and re-layouts  2.02 us (1%)
    pallas_call x1, Pallas kernels, panels(): pl.pallas_call(panels_kernel, out_shape=(jax.ShapeDtypeStruct((2, 8, CHUN...  132 us
    pallas_call x1, Pallas kernels, update(): pl.pallas_call(update_kernel, grid=(2 * BLOCKS,), out_shape=(jax.ShapeDty...  20.6 us

profile of v3, /device:TPU:0, one launch (start us, length us, event | category | flops | bytes accessed | tf_op | source)
XLA Modules:
  0.0 155.5 jit_solution(11244252536863880811)
XLA Ops:
  0.6 0.0 copy-start
  0.6 1.1 copy-done
  1.7 0.0 copy-start.1
  1.7 1.0 copy-done.1
  2.7 0.0 copy-start.2
  2.7 132.1 %panels.1 = (f32[2,8,64,1152]{3,2,1,0:T(8,128)}, f32[8,64,1152]{2,1,0:T(8,128)S(1)}, f32[512,512]{1,0:T(8,128)S(1)}, f32[512,512]{1,0:T(8,128)S(1)}, f32[8,128]{1,0:T(8,128)S(1)}, /*index=5*/f32[512,128]{1,0:T(8,128)S(1)}) custom-call(f32[144,512]{1,0:T(8,128)S(1)} %copy-done.1, f32[1152,128]{1,0:T(8,128)S(1)} %copy-done, f32[1152,2304]{1,0:T(8,128)} %r_ref.3), custom_call_target="tpu_custom_call" | custom-call | tf_op jit(solution)/shard_map/panels/pallas_call | solution.py:428
  134.7 0.0 copy-done.2
  134.7 20.6 %update.1 = (f32[1152,2304]{1,0:T(8,128)}, f32[1152,128]{1,0:T(8,128)}) custom-call(f32[512,512]{1,0:T(8,128)S(1)} %get-tuple-element.8.a_ref, f32[512,512]{1,0:T(8,128)S(1)} %get-tuple-element.9.g_ref, f32[8,128]{1,0:T(8,128)S(1)} %get-tuple-element.10.size_ref, f32[512,1152]{1,0:T(8,128)S(1)} %bitcast.3, f32[2,512,1152]{2,1,0:T(8,128)} %bitcast.5, ...), custom_call_target="tpu_custom_call" | custom-call | tf_op jit(solution)/shard_map/update/pallas_call | solution.py:513
Async XLA Ops:
  0.6 1.1 copy-start
  1.7 1.0 copy-start.1
  2.7 132.1 %copy-start.2 = (s32[512]{0:T(512)S(1)}, s32[512]{0:T(512)}, u32[]{:S(2)}) copy-start(s32[512]{0:T(512)} %param.5) | copy-start | bytes 6148

commit v4 on v3

--- a/solution.py
+++ b/solution.py
@@ -50,11 +50,10 @@
         self.inner = y_hi != y_lo
         self.off_diagonal = x != z
         between = lax.rem(y_hi + y_lo, 2)
-        far_y, near_y = lax.rem(y_hi + between, 2), lax.rem(y_lo + 1 - between, 2)
-        self.sum_to = ((far_y * 4 + x) * 2 + core, near_y * 4 + z)
         back_y, side_y = lax.rem(y_hi + 1 - between, 2), lax.rem(y_lo + between, 2)
         self.spread_to = ((back_y * 4 + x) * 2 + core, side_y * 4 + z)
-        self.spread_slot = far_y * 4 + x
+        self.spread_slot = lax.rem(y_hi + between, 2) * 4 + x
+        self.sum_to = [((y_lo * 4 + x) * 2 + core, part * 4 + z) for part in range(2)]
 
 
 class Copies:
@@ -67,9 +66,10 @@
         self.count += 1
         return self.count - 1
 
-    def make(self, index, src, dst, device):
+    def make(self, index, src, dst, device, recv=None):
+        recv = index if recv is None else recv
         return pltpu.make_async_remote_copy(
-            src_ref=src, dst_ref=dst, send_sem=self.send_sems.at[index], recv_sem=self.recv_sems.at[index],
+            src_ref=src, dst_ref=dst, send_sem=self.send_sems.at[index], recv_sem=self.recv_sems.at[recv],
             device_id=device, device_id_type=MESH)
 
     def start(self, src, dst, device):
@@ -186,10 +186,11 @@
 
 BLOCKS = 3
 BLOCK = 384
+PART = 256
 
 
 def panels_kernel(x_ref, w_ref, r_ref, uc_ref, ur_ref, a_ref, g_ref, size_ref, fit_ref,
-                  wv, rv, xr, xs, part, from_sib, acc, ra, rb, ry, ry2, relay, s_all, sp, rs0, sh, rs1, sh2, rs2,
+                  wv, rv, xr, xs, part, from_sib, acc, ra, rb, ry, relay, s_all, sp, rs0, sh, rs1, sh2, rs2,
                   fx, rf0, fh, rf1, fh2, rf2, local_sems, send_sems, recv_sems):
     at = Place()
     k, p, col = at.core, at.chip_row, at.col
@@ -199,9 +200,11 @@
     def columns(h, j):
         return pl.ds(pl.multiple_of((h * BLOCKS + j) * BLOCK, 128), BLOCK)
 
-    own_x = pltpu.make_async_copy(x_ref, xr.at[col], local_sems.at[2 * BLOCKS])
-    own_x.start()
-    own_w = pltpu.make_async_copy(w_ref, wv, local_sems.at[2 * BLOCKS + 1])
+    own_x = [pltpu.make_async_copy(x_ref.at[:, pl.ds(e * PART, PART)], xr.at[e, col], local_sems.at[2 * BLOCKS + e])
+             for e in range(2)]
+    for copy in own_x:
+        copy.start()
+    own_w = pltpu.make_async_copy(w_ref, wv, local_sems.at[2 * BLOCKS + 2])
     own_w.start()
     loads = []
     for i, (h, j) in enumerate(turns):
@@ -209,105 +212,153 @@
         loads[-1].start()
     greet([at.sibling, at.x_up, at.x_down, at.x_far, at.y_far, at.z_up, at.z_down, at.y_near],
           [(at.inner, at.y_next), (at.off_diagonal, at.swapped)])
-    own_x.wait()
+    for copy in own_x:
+        copy.wait()
     copies = Copies(send_sems, recv_sems)
 
-    gx = Gather(copies, xr, at.y_lo, at.z, at.y_near, at.z_up, at.z_down, rows)
-    gx.own()
-    gx.forward_own()
-    gx.pair_across()
-    gx.far_own()
-    gx.far_by_pair()
-    gx.end_by_pair()
-    stack_left(xs, xr[...].reshape(8 * rows, ALL).T)
+    ga, gb = (Gather(copies, xr.at[e], at.y_lo, at.z, at.y_near, at.z_up, at.z_down, rows) for e in range(2))
+    ga.own()
+    ga.forward_own()
+    ga.pair_across()
+    ga.far_own()
+    ga.far_by_pair()
+    gb.own()
+    ga.end_by_pair()
+
+    def stack_features(e):
+        stack_left(xs.at[pl.ds(e * PART, PART)], xr[e].reshape(8 * rows, PART).T)
+
+    def product(e, i):
+        h, j = turns[i]
+        if e == 0:
+            loads[i].wait()
+        value = mm(xs[e * PART:(e + 1) * PART], stack_right(rv[i]))
+        part[h, 4 * e:4 * e + 4, :, j * BLOCK:(j + 1) * BLOCK] = value.reshape(4, CHUNK, BLOCK)
+
+    sib = {}
+
+    def part_to_sibling(e, j):
+        piece = (pl.ds(4 * e, 4), slice(None), slice(j * BLOCK, (j + 1) * BLOCK))
+        sib[e, j] = copies.start(part.at[(1 - k,) + piece], from_sib.at[piece], at.sibling)
+
+    half = CHUNK // 2
+    low, high = pl.ds(0, half), pl.ds(half, half)
+    a_up, a_down, b_up, b_down = {}, {}, {}, {}
+
+    def chunk(e, x_step):
+        return e * 4 + lax.rem(at.x + x_step, 4)
+
+    def scatter_far(e):
+        for j in range(BLOCKS):
+            copies.arrived(sib[e, j], from_sib.at[pl.ds(4 * e, 4), :, j * BLOCK:(j + 1) * BLOCK], at.sibling)
+        for x_step in (2, 1, 3, 0):
+            ch = chunk(e, x_step)
+            acc[ch] = part[k, ch] + from_sib[ch]
+            if x_step == 2:
+                a_up[e] = copies.start(acc.at[ch, low], ra.at[0, e], at.x_up)
+                a_down[e] = copies.start(acc.at[ch, high], ra.at[1, e], at.x_down)
+
+    def scatter_near(e):
+        ch = chunk(e, 1)
+        copies.arrived(a_up[e], ra.at[0, e], at.x_down)
+        acc[ch, low] = acc[ch, low] + ra[0, e]
+        b_up[e] = copies.start(acc.at[ch], rb.at[0, e], at.x_up)
+        ch = chunk(e, 3)
+        copies.arrived(a_down[e], ra.at[1, e], at.x_up)
+        acc[ch, high] = acc[ch, high] + ra[1, e]
+        b_down[e] = copies.start(acc.at[ch], rb.at[1, e], at.x_down)
+
+    y_sems = [copies.take() for _ in range(2)]
+
+    def sum_copy(e):
+        return copies.make(y_sems[e], acc.at[chunk(e, 0)], ry.at[at.y_hi], at.sum_to[e], y_sems[0] + at.y_hi)
+
+    def stays(e):
+        return (at.y_hi == e) & (at.y_lo == e)
+
+    def scatter_end(e):
+        ch = chunk(e, 0)
+        copies.arrived(b_up[e], rb.at[0, e], at.x_down)
+        copies.arrived(b_down[e], rb.at[1, e], at.x_up)
+        acc[ch] = acc[ch] + (rb[0, e] + rb[1, e])
+
+        @pl.when(jnp.logical_not(stays(e)))
+        def _():
+            sum_copy(e).start()
+
+    stack_features(0)
+    product(0, 0)
+    part_to_sibling(0, 0)
+    product(0, 1)
+    part_to_sibling(0, 1)
+    gb.forward_own()
+    product(0, 2)
+    part_to_sibling(0, 2)
+    product(0, 3)
+    gb.pair_across()
+    product(0, 4)
+    product(0, 5)
+    scatter_far(0)
+    gb.far_own()
+    gb.far_by_pair()
+    gb.end_by_pair()
+    stack_features(1)
+    product(1, 0)
+    part_to_sibling(1, 0)
+    scatter_near(0)
 
     own_w.wait()
     fx[...] = mm(xs[...], stack_right(wv[...]))
     n = ALL // 2
+    quarter = n // 4
     f0 = copies.start(fx.at[pl.ds(pl.multiple_of((1 - k) * n, n), n)], rf0, at.sibling)
-
-    def product(i):
-        h, j = turns[i]
-        loads[i].wait()
-        value = mm(xs[...], stack_right(rv[i]))
-        part[h, :, :, j * BLOCK:(j + 1) * BLOCK] = value.reshape(8, CHUNK, BLOCK)
-
-    sib = []
-    for j in range(BLOCKS):
-        product(j)
-        piece = (slice(None), slice(None), slice(j * BLOCK, (j + 1) * BLOCK))
-        sib.append(copies.start(part.at[(1 - k,) + piece], from_sib.at[piece], at.sibling))
-        if j == 0:
-            copies.arrived(f0, rf0, at.sibling)
-            fh[...] = fx[pl.ds(pl.multiple_of(k * n, n), n)] + rf0[...]
-            f1 = [copies.start(fh, rf1.at[i], d) for i, d in enumerate((at.x_up, at.x_down, at.x_far))]
-    for j in range(BLOCKS):
-        product(BLOCKS + j)
-    for j in range(BLOCKS):
-        copies.arrived(sib[j], from_sib.at[:, :, j * BLOCK:(j + 1) * BLOCK], at.sibling)
-
-    def chunk(y_step, x_step):
-        y = at.y_hi if y_step == 0 else 1 - at.y_hi
-        return y * 4 + lax.rem(at.x + x_step, 4)
-
-    def add_sibling(y, x_step):
-        ch = chunk(y, x_step)
-        acc[ch] = part[k, ch] + from_sib[ch]
-        return ch
-
-    half = CHUNK // 2
-    low, high = pl.ds(0, half), pl.ds(half, half)
-    a_up, a_down, b_up, b_down = {}, {}, {}, {}
-    for y in (1, 0):
-        ch = add_sibling(y, 2)
-        a_up[y] = copies.start(acc.at[ch, low], ra.at[0, y], at.x_up)
-        a_down[y] = copies.start(acc.at[ch, high], ra.at[1, y], at.x_down)
-    for y in (1, 0):
-        for x_step in (1, 3, 0):
-            add_sibling(y, x_step)
+    product(1, 1)
+    part_to_sibling(1, 1)
+    product(1, 2)
+    part_to_sibling(1, 2)
+    copies.arrived(f0, rf0, at.sibling)
+    fh[...] = fx[pl.ds(pl.multiple_of(k * n, n), n)] + rf0[...]
+
+    def quarter_at(x_step, base=0):
+        return pl.ds(pl.multiple_of(base + lax.rem(at.x + x_step, 4) * quarter, quarter), quarter)
+
+    steps = ((1, at.x_up), (3, at.x_down), (2, at.x_far))
+    f1 = [copies.start(fh.at[quarter_at(t)], rf1.at[i], d) for i, (t, d) in enumerate(steps)]
+    product(1, 3)
+    product(1, 4)
+    product(1, 5)
+    scatter_far(1)
+    scatter_end(0)
     for i, d in enumerate((at.x_down, at.x_up, at.x_far)):
         copies.arrived(f1[i], rf1.at[i], d)
-    fh2[...] = (fh[...] + rf1[2]) + (rf1[0] + rf1[1])
+    fh2[...] = (fh[quarter_at(0)] + rf1[2]) + (rf1[0] + rf1[1])
     f2 = copies.start(fh2, rf2, at.y_far)
-    for y in (1, 0):
-        ch = chunk(y, 1)
-        copies.arrived(a_up[y], ra.at[0, y], at.x_down)
-        acc[ch, low] = acc[ch, low] + ra[0, y]
-        b_up[y] = copies.start(acc.at[ch], rb.at[0, y], at.x_up)
-        ch = chunk(y, 3)
-        copies.arrived(a_down[y], ra.at[1, y], at.x_up)
-        acc[ch, high] = acc[ch, high] + ra[1, y]
-        b_down[y] = copies.start(acc.at[ch], rb.at[1, y], at.x_down)
-
-    def add_x(y):
-        ch = chunk(y, 0)
-        copies.arrived(b_up[y], rb.at[0, y], at.x_down)
-        copies.arrived(b_down[y], rb.at[1, y], at.x_up)
-        return acc[ch] + (rb[0, y] + rb[1, y])
-
-    other, own = chunk(1, 0), chunk(0, 0)
-    acc[other] = add_x(1)
-    c1 = copies.start(acc.at[other], ry, at.sum_to)
-    acc[own] = add_x(0)
-    c2 = copies.take()
-    inner_sum = copies.make(c2, acc.at[own], ry2, at.y_next)
+    scatter_near(1)
+    copies.arrived(f2, rf2, at.y_far)
+    fit_own = fit_ref.at[quarter_at(0, k * n)]
+    fit_own[...] = fh2[...] + rf2[...]
+    f3 = [copies.start(fit_own, fit_own, d) for _, d in steps]
+    scatter_end(1)
+
+    own = at.y_hi * 4 + at.x
 
     @pl.when(at.inner)
     def _():
-        inner_sum.start()
-
-    copies.arrived(c1, ry, at.sum_to)
-
-    @pl.when(at.inner)
-    def _():
-        copies.make(c2, ry2, ry2, at.y_next).wait_recv()
-        relay[...] = ry[...] + ry2[...]
-        inner_sum.wait_send()
+        for i in range(2):
+            copies.make(y_sems[0], ry.at[i], ry.at[i], at.y_next, y_sems[i]).wait_recv()
+        relay[...] = ry[0] + ry[1]
 
     @pl.when(jnp.logical_not(at.inner))
     def _():
-        relay[...] = acc[own] + ry[...]
+        there = 1 - at.y_hi
+        copies.make(y_sems[0], ry.at[there], ry.at[there], at.y_far, y_sems[0] + there).wait_recv()
+        relay[...] = acc[own] + ry[there]
         uc_ref[k, p] = relay[...]
+
+    for e in range(2):
+        @pl.when(jnp.logical_not(stays(e)))
+        def _():
+            sum_copy(e).wait_send()
 
     t1 = copies.take()
     step_xz = copies.make(t1, relay, ur_ref.at[at.y_lo * 4 + at.x], at.swapped)
@@ -333,10 +384,10 @@
         piece = gc.part(pair_step, ring_step)
         return copies.start(piece, piece, at.sibling)
 
-    copies.arrived(f2, rf2, at.y_far)
-    mine_fit = fit_ref.at[pl.ds(pl.multiple_of(k * n, n), n)]
-    mine_fit[...] = fh2[...] + rf2[...]
-    f3 = copies.start(mine_fit, mine_fit, at.sibling)
+    for f, t, d in zip(f3, (3, 1, 2), (at.x_down, at.x_up, at.x_far)):
+        copies.arrived(f, fit_ref.at[quarter_at(t, k * n)], d)
+    fit_half = fit_ref.at[pl.ds(pl.multiple_of(k * n, n), n)]
+    f4 = copies.start(fit_half, fit_half, at.sibling)
 
     @pl.when(at.inner)
     def _():
@@ -357,7 +408,9 @@
 
     gr.own()
 
-    sp[...] = dot3(split(ur_ref[col]), split(xr[...].reshape(8 * rows, ALL)))
+    left = split(ur_ref[col])
+    for e in range(2):
+        sp[:, e * PART:(e + 1) * PART] = dot3(left, split(xr[e].reshape(8 * rows, PART)))
     s0 = copies.start(sp.at[pl.ds(pl.multiple_of((1 - k) * half, half), half)], rs0, at.sibling)
     copies.arrived(s0, rs0, at.sibling)
     sh[...] = sp[pl.ds(pl.multiple_of(k * half, half), half)] + rs0[...]
@@ -414,7 +467,7 @@
     other_block = uc_ref.at[1 - k]
     for (pair_step, ring_step), index in u.items():
         copies.arrived(index, other_block.at[gc.slot(pair_step, ring_step)], at.sibling)
-    copies.arrived(f3, fit_ref.at[pl.ds(pl.multiple_of((1 - k) * n, n), n)], at.sibling)
+    copies.arrived(f4, fit_ref.at[pl.ds(pl.multiple_of((1 - k) * n, n), n)], at.sibling)
     copies.finish()
 
 
@@ -440,15 +493,14 @@
         scratch_shapes=[
             pltpu.VMEM(head.shape, F32),
             pltpu.VMEM((2 * BLOCKS, depth, BLOCK), F32),
-            pltpu.VMEM((8, rows, examples), F32),
+            pltpu.VMEM((2, 8, rows, PART), F32),
             pltpu.VMEM((examples, 3 * depth), BF16),
             pltpu.VMEM((2, 8, CHUNK, width), F32),
             pltpu.VMEM((8, CHUNK, width), F32),
             pltpu.VMEM((8, CHUNK, width), F32),
             pltpu.VMEM((2, 2, half, width), F32),
             pltpu.VMEM((2, 2, CHUNK, width), F32),
-            pltpu.VMEM((CHUNK, width), F32),
-            pltpu.VMEM((CHUNK, width), F32),
+            pltpu.VMEM((2, CHUNK, width), F32),
             pltpu.VMEM((CHUNK, width), F32),
             pltpu.VMEM((2, 8, half, ALL), F32),
             pltpu.VMEM((CHUNK, ALL), F32),
@@ -460,12 +512,12 @@
             pltpu.VMEM((ALL, classes), F32),
             pltpu.VMEM((ALL // 2, classes), F32),
             pltpu.VMEM((ALL // 2, classes), F32),
-            pltpu.VMEM((3, ALL // 2, classes), F32),
-            pltpu.VMEM((ALL // 2, classes), F32),
-            pltpu.VMEM((ALL // 2, classes), F32),
-            dma((2 * BLOCKS + 2,)),
-            dma((80,)),
-            dma((80,)),
+            pltpu.VMEM((3, ALL // 8, classes), F32),
+            pltpu.VMEM((ALL // 8, classes), F32),
+            pltpu.VMEM((ALL // 8, classes), F32),
+            dma((2 * BLOCKS + 3,)),
+            dma((96,)),
+            dma((96,)),
         ],
         compiler_params=pltpu.CompilerParams(collective_id=0, has_side_effects=True, vmem_limit_bytes=VMEM_PANELS),
         name="panels",

time: 157 us -> 144 us (0.917)
  Pallas kernels: 153 us -> 139 us
    pallas_call x1, Pallas kernels: 132 us -> 115 us  [panels(): pl.pallas_call(panels_kernel, out_shape=(jax.ShapeDtypeStruct((2, 8, CHUN...]
    pallas_call x1, Pallas kernels: 20.6 us -> 23.5 us  [update(): pl.pallas_call(update_kernel, grid=(2 * BLOCKS,), out_shape=(jax.ShapeDty...]
where the time goes in v4:
time: 144 us; the launch traced here: 142 us
  Pallas kernels  139 us (97%)
  local copies, waits for them, and re-layouts  2.02 us (1%)
    pallas_call x1, Pallas kernels, panels(): pl.pallas_call(panels_kernel, out_shape=(jax.ShapeDtypeStruct((2, 8, CHUN...  115 us
    pallas_call x1, Pallas kernels, update(): pl.pallas_call(update_kernel, grid=(2 * BLOCKS,), out_shape=(jax.ShapeDty...  23.5 us

profile of v4, /device:TPU:0, one launch (start us, length us, event | category | flops | bytes accessed | tf_op | source)
XLA Modules:
  0.0 141.7 jit_solution(1705137581825916597)
XLA Ops:
  0.6 0.0 copy-start
  0.6 1.1 copy-done
  1.7 0.0 copy-start.1
  1.7 1.0 copy-done.1
  2.7 0.0 copy-start.2
  2.7 115.4 %panels.1 = (f32[2,8,64,1152]{3,2,1,0:T(8,128)}, f32[8,64,1152]{2,1,0:T(8,128)S(1)}, f32[512,512]{1,0:T(8,128)S(1)}, f32[512,512]{1,0:T(8,128)S(1)}, f32[8,128]{1,0:T(8,128)S(1)}, /*index=5*/f32[512,128]{1,0:T(8,128)S(1)}) custom-call(f32[144,512]{1,0:T(8,128)S(1)} %copy-done.1, f32[1152,128]{1,0:T(8,128)S(1)} %copy-done, f32[1152,2304]{1,0:T(8,128)} %r_ref.3), custom_call_target="tpu_custom_call" | custom-call | tf_op jit(solution)/shard_map/panels/pallas_call | solution.py:481
  118.0 0.0 copy-done.2
  118.0 23.5 %update.1 = (f32[1152,2304]{1,0:T(8,128)}, f32[1152,128]{1,0:T(8,128)}) custom-call(f32[512,512]{1,0:T(8,128)S(1)} %get-tuple-element.8.a_ref, f32[512,512]{1,0:T(8,128)S(1)} %get-tuple-element.9.g_ref, f32[8,128]{1,0:T(8,128)S(1)} %get-tuple-element.10.size_ref, f32[512,1152]{1,0:T(8,128)S(1)} %bitcast.3, f32[2,512,1152]{2,1,0:T(8,128)} %bitcast.5, ...), custom_call_target="tpu_custom_call" | custom-call | tf_op jit(solution)/shard_map/update/pallas_call | solution.py:565
Async XLA Ops:
  0.6 1.1 copy-start
  1.7 1.0 copy-start.1
  2.7 115.4 %copy-start.2 = (s32[512]{0:T(512)S(1)}, s32[512]{0:T(512)}, u32[]{:S(2)}) copy-start(s32[512]{0:T(512)} %param.5) | copy-start | bytes 6148

commit v5 on v4

--- a/solution.py
+++ b/solution.py
@@ -11,8 +11,8 @@
 ALL = 512
 CHUNK = 64
 MIB = 1 << 20
-VMEM_PANELS = 48 * MIB
-VMEM_UPDATE = 48 * MIB
+VMEM_PANELS = 44 * MIB
+VMEM_UPDATE = 30 * MIB
 
 
 def split(value):
@@ -124,6 +124,9 @@
 
     def own(self):
         self.own_ring()
+        self.own_pair()
+
+    def own_pair(self):
         self.i_pair = self.same(self.part(0, 0), self.pair)
 
     def own_ring(self):
@@ -190,7 +193,7 @@
 
 
 def panels_kernel(x_ref, w_ref, r_ref, uc_ref, ur_ref, a_ref, g_ref, size_ref, fit_ref,
-                  wv, rv, xr, xs, part, from_sib, acc, ra, rb, ry, relay, s_all, sp, rs0, sh, rs1, sh2, rs2,
+                  wv, rv, xr, xs, part, from_sib, acc, ra, rb, ry, relay, xh, xl, s_all, sp, rs0, sh, rs1, sh2, rs2,
                   fx, rf0, fh, rf1, fh2, rf2, local_sems, send_sems, recv_sems):
     at = Place()
     k, p, col = at.core, at.chip_row, at.col
@@ -389,57 +392,60 @@
     fit_half = fit_ref.at[pl.ds(pl.multiple_of(k * n, n), n)]
     f4 = copies.start(fit_half, fit_half, at.sibling)
 
+    for e in range(2):
+        hi, lo = split(xr[e].reshape(8 * rows, PART))
+        xh[:, e * PART:(e + 1) * PART] = hi
+        xl[:, e * PART:(e + 1) * PART] = lo
+
+    @pl.when(at.off_diagonal)
+    def _():
+        copies.make(t1, ur_ref.at[col], ur_ref.at[col], at.swapped).wait_recv()
+        step_xz.wait_send()
+
+    @pl.when(jnp.logical_not(at.off_diagonal))
+    def _():
+        ur_ref[col] = relay[...]
+
+    gr.own_ring()
+
+    sp[...] = dot3(split(ur_ref[col]), (xh[...], xl[...]))
+    s0 = copies.start(sp.at[pl.ds(pl.multiple_of((1 - k) * half, half), half)], rs0, at.sibling)
+
     @pl.when(at.inner)
     def _():
         copies.make(d2, uc_ref.at[k, p], uc_ref.at[k, p], at.y_next).wait_recv()
         inner_back.wait_send()
 
-    gc.own_ring()
-    u = {(0, 0): to_sibling(0, 0)}
-
-    @pl.when(at.off_diagonal)
-    def _():
-        copies.make(t1, ur_ref.at[col], ur_ref.at[col], at.swapped).wait_recv()
-        step_xz.wait_send()
-
-    @pl.when(jnp.logical_not(at.off_diagonal))
-    def _():
-        ur_ref[col] = relay[...]
-
-    gr.own()
-
-    left = split(ur_ref[col])
-    for e in range(2):
-        sp[:, e * PART:(e + 1) * PART] = dot3(left, split(xr[e].reshape(8 * rows, PART)))
-    s0 = copies.start(sp.at[pl.ds(pl.multiple_of((1 - k) * half, half), half)], rs0, at.sibling)
     copies.arrived(s0, rs0, at.sibling)
     sh[...] = sp[pl.ds(pl.multiple_of(k * half, half), half)] + rs0[...]
     s1 = [copies.start(sh, rs1.at[i], d) for i, d in enumerate((at.x_up, at.x_down, at.x_far))]
+    u = {(0, 0): to_sibling(0, 0)}
     for i, d in enumerate((at.x_down, at.x_up, at.x_far)):
         copies.arrived(s1[i], rs1.at[i], d)
     sh2[...] = (sh[...] + rs1[2]) + (rs1[0] + rs1[1])
     s2 = copies.start(sh2, rs2, at.y_far)
+    gc.own_ring()
+    copies.arrived(s2, rs2, at.y_far)
+    s_all[k, col] = sh2[...] + rs2[...]
+    gs = Gather(copies, s_all.at[k], at.y_lo, at.z, at.y_near, at.z_up, at.z_down, half)
+    gs.own()
+    gr.own_pair()
+    gs.forward_own()
+    gs.pair_across()
+    gr.forward_own()
     gc.forward_own()
     gc.pair_across()
     for step in ((0, 3), (0, 1), (1, 0)):
         u[step] = to_sibling(*step)
-    copies.arrived(s2, rs2, at.y_far)
-    s_all[k, col] = sh2[...] + rs2[...]
-    gs = Gather(copies, s_all.at[k], at.y_lo, at.z, at.y_near, at.z_up, at.z_down, half)
-    gs.own()
-    gs.forward_own()
-    gs.pair_across()
     gs.far_own()
     gs.forward_pair()
     gs.end_by_ring()
     s4 = copies.start(s_all.at[k], s_all.at[k], at.sibling)
-    gr.forward_own()
     gr.pair_across()
+    gr.far_own()
+    gr.far_by_pair()
     gc.far_own()
     u[(0, 2)] = to_sibling(0, 2)
-    gc.forward_pair()
-    for step in ((1, 3), (1, 1)):
-        u[step] = to_sibling(*step)
     copies.arrived(s4, s_all.at[1 - k], at.sibling)
 
     for c in range(8):
@@ -457,10 +463,11 @@
         g_ref[...] = g_ref[...] + dot3(g, split(error))
         size_ref[...] = jnp.broadcast_to(jnp.sum(error * error), size_ref.shape)
 
-    pl.loop(0, 2)(refine)
-    gr.far_own()
-    gr.far_by_pair()
-    pl.loop(0, 2)(refine)
+    pl.loop(0, 3)(refine)
+    gc.forward_pair()
+    for step in ((1, 3), (1, 1)):
+        u[step] = to_sibling(*step)
+    pl.loop(0, 1)(refine)
     gc.end_by_ring()
     u[(1, 2)] = to_sibling(1, 2)
     gr.end_by_pair()
@@ -502,6 +509,8 @@
             pltpu.VMEM((2, 2, CHUNK, width), F32),
             pltpu.VMEM((2, CHUNK, width), F32),
             pltpu.VMEM((CHUNK, width), F32),
+            pltpu.VMEM((depth, examples), BF16),
+            pltpu.VMEM((depth, examples), BF16),
             pltpu.VMEM((2, 8, half, ALL), F32),
             pltpu.VMEM((CHUNK, ALL), F32),
             pltpu.VMEM((half, ALL), F32),

time: 144 us -> 143 us (level)
  Pallas kernels: 139 us -> 134 us
  local copies, waits for them, and re-layouts: 2.02 us -> 6.03 us
    pallas_call x1, Pallas kernels: 115 us -> 111 us  [panels(): pl.pallas_call(panels_kernel, out_shape=(jax.ShapeDtypeStruct((2, 8, CHUN...]
    unnamed x6 -> x8, local copies, waits for them, and re-layouts: 2.02 us -> 6.03 us
where the time goes in v5:
time: 143 us; the launch traced here: 141 us
  Pallas kernels  134 us (94%)
  local copies, waits for them, and re-layouts  6.03 us (4%)
    pallas_call x1, Pallas kernels, panels(): pl.pallas_call(panels_kernel, out_shape=(jax.ShapeDtypeStruct((2, 8, CHUN...  111 us
    pallas_call x1, Pallas kernels, update(): pl.pallas_call(update_kernel, grid=(2 * BLOCKS,), out_shape=(jax.ShapeDty...  23.4 us
    unnamed x8, local copies, waits for them, and re-layouts  6.03 us

profile of v5, /device:TPU:0, one launch (start us, length us, event | category | flops | bytes accessed | tf_op | source)
XLA Modules:
  0.0 141.2 jit_solution(1266038559657660538)
XLA Ops:
  0.6 0.0 copy-start.1
  0.6 1.1 copy-done.1
  1.7 0.0 copy-start.2
  1.7 1.0 copy-done.2
  2.7 0.0 copy-start.3
  2.7 111.0 %panels.1 = (f32[2,8,64,1152]{3,2,1,0:T(8,128)S(1)}, f32[8,64,1152]{2,1,0:T(8,128)S(1)}, f32[512,512]{1,0:T(8,128)S(1)}, f32[512,512]{1,0:T(8,128)S(1)}, f32[8,128]{1,0:T(8,128)S(1)}, /*index=5*/f32[512,128]{1,0:T(8,128)S(1)}) custom-call(f32[144,512]{1,0:T(8,128)S(1)} %copy-done.2, f32[1152,128]{1,0:T(8,128)S(1)} %copy-done.1, f32[1152,2304]{1,0:T(8,128)} %r_ref.3), custom_call_target="tpu_custom_call" | custom-call | tf_op jit(solution)/shard_map/panels/pallas_call | solution.py:488
  113.7 0.0 copy-done.3
  113.7 0.0 copy-start
  113.7 4.0 %copy-done = f32[1152,2304]{1,0:T(8,128)S(1)} copy-done((f32[1152,2304]{1,0:T(8,128)S(1)}, f32[1152,2304]{1,0:T(8,128)}, u32[]{:S(2)}) %copy-start) | copy-done | bytes 10616856
  117.7 23.4 %update.1 = (f32[1152,2304]{1,0:T(8,128)}, f32[1152,128]{1,0:T(8,128)}) custom-call(f32[512,512]{1,0:T(8,128)S(1)} %get-tuple-element.8.a_ref, f32[512,512]{1,0:T(8,128)S(1)} %get-tuple-element.9.g_ref, f32[8,128]{1,0:T(8,128)S(1)} %get-tuple-element.10.size_ref, f32[512,1152]{1,0:T(8,128)S(1)} %bitcast.4, f32[2,512,1152]{2,1,0:T(8,128)S(1)} %bitcast.3, ...), custom_call_target="tpu_custom_call" | custom-call | tf_op jit(solution)/shard_map/update/pallas_call | solution.py:574
Async XLA Ops:
  0.6 1.1 copy-start.1
  1.7 1.0 copy-start.2
  2.7 111.0 %copy-start.3 = (s32[512]{0:T(512)S(1)}, s32[512]{0:T(512)}, u32[]{:S(2)}) copy-start(s32[512]{0:T(512)} %param.5) | copy-start | bytes 6148
  113.7 4.0 %copy-start = (f32[1152,2304]{1,0:T(8,128)S(1)}, f32[1152,2304]{1,0:T(8,128)}, u32[]{:S(2)}) copy-start(f32[1152,2304]{1,0:T(8,128)} %r_ref.3) | copy-start | bytes 31850500

commit v6 on v5

--- a/solution.py
+++ b/solution.py
@@ -12,7 +12,7 @@
 CHUNK = 64
 MIB = 1 << 20
 VMEM_PANELS = 44 * MIB
-VMEM_UPDATE = 30 * MIB
+VMEM_UPDATE = 34 * MIB
 
 
 def split(value):
@@ -193,7 +193,7 @@
 
 
 def panels_kernel(x_ref, w_ref, r_ref, uc_ref, ur_ref, a_ref, g_ref, size_ref, fit_ref,
-                  wv, rv, xr, xs, part, from_sib, acc, ra, rb, ry, relay, xh, xl, s_all, sp, rs0, sh, rs1, sh2, rs2,
+                  wv, rv, xr, xs, part, from_sib, ra, rb, ry, relay, xh, xl, s_all, sp, rs0, sh, rs1, sh2, rs2,
                   fx, rf0, fh, rf1, fh2, rf2, local_sems, send_sems, recv_sems):
     at = Place()
     k, p, col = at.core, at.chip_row, at.col
@@ -238,6 +238,7 @@
         value = mm(xs[e * PART:(e + 1) * PART], stack_right(rv[i]))
         part[h, 4 * e:4 * e + 4, :, j * BLOCK:(j + 1) * BLOCK] = value.reshape(4, CHUNK, BLOCK)
 
+    acc = part.at[k]
     sib = {}
 
     def part_to_sibling(e, j):
@@ -256,7 +257,7 @@
             copies.arrived(sib[e, j], from_sib.at[pl.ds(4 * e, 4), :, j * BLOCK:(j + 1) * BLOCK], at.sibling)
         for x_step in (2, 1, 3, 0):
             ch = chunk(e, x_step)
-            acc[ch] = part[k, ch] + from_sib[ch]
+            acc[ch] = acc[ch] + from_sib[ch]
             if x_step == 2:
                 a_up[e] = copies.start(acc.at[ch, low], ra.at[0, e], at.x_up)
                 a_down[e] = copies.start(acc.at[ch, high], ra.at[1, e], at.x_down)
@@ -504,7 +505,6 @@
             pltpu.VMEM((examples, 3 * depth), BF16),
             pltpu.VMEM((2, 8, CHUNK, width), F32),
             pltpu.VMEM((8, CHUNK, width), F32),
-            pltpu.VMEM((8, CHUNK, width), F32),
             pltpu.VMEM((2, 2, half, width), F32),
             pltpu.VMEM((2, 2, CHUNK, width), F32),
             pltpu.VMEM((2, CHUNK, width), F32),
@@ -530,7 +530,9 @@
         ],
         compiler_params=pltpu.CompilerParams(collective_id=0, has_side_effects=True, vmem_limit_bytes=VMEM_PANELS),
         name="panels",
-    )(features_t, head, tile)
+    )(pltpu.with_memory_space_constraint(features_t, pltpu.HBM),
+      pltpu.with_memory_space_constraint(head, pltpu.HBM),
+      pltpu.with_memory_space_constraint(tile, pltpu.HBM))
 
 
 def update_kernel(a_ref, g_ref, size_ref, ur_ref, u_ref, r_ref, labels_ref, fit_ref, w_ref, out_ref, head_ref,
@@ -565,7 +567,8 @@
         head_ref[...] = w_ref[...] + mm(gain_ref[...], stack_right(targets - fit_ref[...]))
 
     load(at).wait()
-    out_ref[...] = rv[at] - mm(gain_ref[...], stack_right(u_ref[0]))
+    block = u_ref[at // BLOCKS, :, pl.ds(pl.multiple_of(lax.rem(at, BLOCKS) * BLOCK, 128), BLOCK)]
+    out_ref[...] = rv[at] - mm(gain_ref[...], stack_right(block))
 
 
 def update(system, inverse, size, rows_t, cols_t, tile, labels, fitted, head):
@@ -576,7 +579,7 @@
         grid=(2 * BLOCKS,),
         out_shape=(jax.ShapeDtypeStruct(tile.shape, F32), jax.ShapeDtypeStruct(head.shape, F32)),
         in_specs=[vmem] * 4 + [
-            pl.BlockSpec((1, ALL, BLOCK), lambda i: (i // BLOCKS, 0, lax.rem(i, BLOCKS))),
+            vmem,
             pl.BlockSpec(memory_space=pl.ANY),
         ] + [vmem] * 3,
         out_specs=(pl.BlockSpec((rows, BLOCK), lambda i: (0, i)), pl.BlockSpec(head.shape, lambda i: (0, 0))),
@@ -588,7 +591,7 @@
         ],
         compiler_params=pltpu.CompilerParams(vmem_limit_bytes=VMEM_UPDATE),
         name="update",
-    )(system, inverse, size, rows_t, cols_t, tile, labels.reshape(1, ALL), fitted, head)
+    )(system, inverse, size, rows_t, cols_t, pltpu.with_memory_space_constraint(tile, pltpu.HBM), labels.reshape(1, ALL), fitted, head)
 
 
 def on_device(features_t, labels, inv_corr, heads):

time: 143 us -> 136 us (0.951)
  local copies, waits for them, and re-layouts: 6.03 us -> 0.01 us
    unnamed x8 -> x4, local copies, waits for them, and re-layouts: 6.03 us -> 0.01 us
where the time goes in v6:
time: 136 us; the launch traced here: 134 us
  Pallas kernels  134 us (99%)
    pallas_call x1, Pallas kernels, panels(): pl.pallas_call(panels_kernel, out_shape=(jax.ShapeDtypeStruct((2, 8, CHUN...  111 us
    pallas_call x1, Pallas kernels, update(): pl.pallas_call(update_kernel, grid=(2 * BLOCKS,), out_shape=(jax.ShapeDty...  22.6 us

profile of v6, /device:TPU:0, one launch (start us, length us, event | category | flops | bytes accessed | tf_op | source)
XLA Modules:
  0.0 134.5 jit_solution(13405558513524232208)
XLA Ops:
  0.6 0.0 copy-start
  0.6 0.0 copy-start.1
  0.6 111.0 %panels.1 = (f32[2,8,64,1152]{3,2,1,0:T(8,128)S(1)}, f32[8,64,1152]{2,1,0:T(8,128)S(1)}, f32[512,512]{1,0:T(8,128)S(1)}, f32[512,512]{1,0:T(8,128)S(1)}, f32[8,128]{1,0:T(8,128)S(1)}, /*index=5*/f32[512,128]{1,0:T(8,128)S(1)}) custom-call(f32[144,512]{1,0:T(8,128)} %x_ref.1, f32[1152,128]{1,0:T(8,128)} %w_ref.3, f32[1152,2304]{1,0:T(8,128)} %r_ref.3), custom_call_target="tpu_custom_call" | custom-call | tf_op jit(solution)/shard_map/panels/pallas_call | solution.py:489
  111.7 0.0 copy-done
  111.7 0.0 copy-done.1
  111.7 22.6 %update.1 = (f32[1152,2304]{1,0:T(8,128)}, f32[1152,128]{1,0:T(8,128)}) custom-call(f32[512,512]{1,0:T(8,128)S(1)} %get-tuple-element.8.a_ref, f32[512,512]{1,0:T(8,128)S(1)} %get-tuple-element.9.g_ref, f32[8,128]{1,0:T(8,128)S(1)} %get-tuple-element.10.size_ref, f32[512,1152]{1,0:T(8,128)S(1)} %bitcast.4, f32[2,512,1152]{2,1,0:T(8,128)S(1)} %bitcast.3, ...), custom_call_target="tpu_custom_call" | custom-call | tf_op jit(solution)/shard_map/update/pallas_call | solution.py:577
Async XLA Ops:
  0.6 111.0 %copy-start = (f32[1152,128]{1,0:T(8,128)S(1)}, f32[1152,128]{1,0:T(8,128)}, u32[]{:S(2)}) copy-start(f32[1152,128]{1,0:T(8,128)} %w_ref.3) | copy-start | bytes 1769476
  0.6 111.0 %copy-start.1 = (s32[512]{0:T(512)S(1)}, s32[512]{0:T(512)}, u32[]{:S(2)}) copy-start(s32[512]{0:T(512)} %param.5) | copy-start | bytes 6148

commit v7 on v6

--- a/solution.py
+++ b/solution.py
@@ -223,9 +223,9 @@
     ga.own()
     ga.forward_own()
     ga.pair_across()
+    gb.own()
     ga.far_own()
     ga.far_by_pair()
-    gb.own()
     ga.end_by_pair()
 
     def stack_features(e):
@@ -291,20 +291,20 @@
             sum_copy(e).start()
 
     stack_features(0)
+    gb.forward_own()
     product(0, 0)
     part_to_sibling(0, 0)
+    gb.pair_across()
     product(0, 1)
     part_to_sibling(0, 1)
-    gb.forward_own()
     product(0, 2)
     part_to_sibling(0, 2)
+    gb.far_own()
+    gb.far_by_pair()
     product(0, 3)
-    gb.pair_across()
     product(0, 4)
     product(0, 5)
     scatter_far(0)
-    gb.far_own()
-    gb.far_by_pair()
     gb.end_by_pair()
     stack_features(1)
     product(1, 0)

time: 136 us -> 138 us (1.015)
  no operation moved by 1% of the time
where the time goes in v7:
time: 138 us; the launch traced here: 136 us
  Pallas kernels  135 us (98%)
    pallas_call x1, Pallas kernels, panels(): pl.pallas_call(panels_kernel, out_shape=(jax.ShapeDtypeStruct((2, 8, CHUN...  112 us
    pallas_call x1, Pallas kernels, update(): pl.pallas_call(update_kernel, grid=(2 * BLOCKS,), out_shape=(jax.ShapeDty...  22.6 us

profile of v7, /device:TPU:0, one launch (start us, length us, event | category | flops | bytes accessed | tf_op | source)
XLA Modules:
  0.0 135.6 jit_solution(4909230991371298363)
XLA Ops:
  0.6 0.0 copy-start
  0.6 0.0 copy-start.1
  0.6 112.1 %panels.1 = (f32[2,8,64,1152]{3,2,1,0:T(8,128)S(1)}, f32[8,64,1152]{2,1,0:T(8,128)S(1)}, f32[512,512]{1,0:T(8,128)S(1)}, f32[512,512]{1,0:T(8,128)S(1)}, f32[8,128]{1,0:T(8,128)S(1)}, /*index=5*/f32[512,128]{1,0:T(8,128)S(1)}) custom-call(f32[144,512]{1,0:T(8,128)} %x_ref.1, f32[1152,128]{1,0:T(8,128)} %w_ref.3, f32[1152,2304]{1,0:T(8,128)} %r_ref.3), custom_call_target="tpu_custom_call" | custom-call | tf_op jit(solution)/shard_map/panels/pallas_call | solution.py:489
  112.8 0.0 copy-done
  112.8 0.0 copy-done.1
  112.8 22.6 %update.1 = (f32[1152,2304]{1,0:T(8,128)}, f32[1152,128]{1,0:T(8,128)}) custom-call(f32[512,512]{1,0:T(8,128)S(1)} %get-tuple-element.8.a_ref, f32[512,512]{1,0:T(8,128)S(1)} %get-tuple-element.9.g_ref, f32[8,128]{1,0:T(8,128)S(1)} %get-tuple-element.10.size_ref, f32[512,1152]{1,0:T(8,128)S(1)} %bitcast.4, f32[2,512,1152]{2,1,0:T(8,128)S(1)} %bitcast.3, ...), custom_call_target="tpu_custom_call" | custom-call | tf_op jit(solution)/shard_map/update/pallas_call | solution.py:577
Async XLA Ops:
  0.6 112.2 %copy-start = (f32[1152,128]{1,0:T(8,128)S(1)}, f32[1152,128]{1,0:T(8,128)}, u32[]{:S(2)}) copy-start(f32[1152,128]{1,0:T(8,128)} %w_ref.3) | copy-start | bytes 1769476
  0.6 112.2 %copy-start.1 = (s32[512]{0:T(512)S(1)}, s32[512]{0:T(512)}, u32[]{:S(2)}) copy-start(s32[512]{0:T(512)} %param.5) | copy-start | bytes 6148

commit v8 on v6

--- a/solution.py
+++ b/solution.py
@@ -464,11 +464,11 @@
         g_ref[...] = g_ref[...] + dot3(g, split(error))
         size_ref[...] = jnp.broadcast_to(jnp.sum(error * error), size_ref.shape)
 
-    pl.loop(0, 3)(refine)
+    pl.loop(0, 1)(refine)
     gc.forward_pair()
     for step in ((1, 3), (1, 1)):
         u[step] = to_sibling(*step)
-    pl.loop(0, 1)(refine)
+    pl.loop(0, 3)(refine)
     gc.end_by_ring()
     u[(1, 2)] = to_sibling(1, 2)
     gr.end_by_pair()

time: 136 us -> 134 us (0.985)
  Pallas kernels: 134 us -> 132 us
    pallas_call x1, Pallas kernels: 111 us -> 109 us  [panels(): pl.pallas_call(panels_kernel, out_shape=(jax.ShapeDtypeStruct((2, 8, CHUN...]
where the time goes in v8:
time: 134 us; the launch traced here: 132 us
  Pallas kernels  132 us (99%)
    pallas_call x1, Pallas kernels, panels(): pl.pallas_call(panels_kernel, out_shape=(jax.ShapeDtypeStruct((2, 8, CHUN...  109 us
    pallas_call x1, Pallas kernels, update(): pl.pallas_call(update_kernel, grid=(2 * BLOCKS,), out_shape=(jax.ShapeDty...  22.6 us

profile of v8, /device:TPU:0, one launch (start us, length us, event | category | flops | bytes accessed | tf_op | source)
XLA Modules:
  0.0 132.4 jit_solution(4632517439771816903)
XLA Ops:
  0.6 0.0 copy-start
  0.6 0.0 copy-start.1
  0.6 108.9 %panels.1 = (f32[2,8,64,1152]{3,2,1,0:T(8,128)S(1)}, f32[8,64,1152]{2,1,0:T(8,128)S(1)}, f32[512,512]{1,0:T(8,128)S(1)}, f32[512,512]{1,0:T(8,128)S(1)}, f32[8,128]{1,0:T(8,128)S(1)}, /*index=5*/f32[512,128]{1,0:T(8,128)S(1)}) custom-call(f32[144,512]{1,0:T(8,128)} %x_ref.1, f32[1152,128]{1,0:T(8,128)} %w_ref.3, f32[1152,2304]{1,0:T(8,128)} %r_ref.3), custom_call_target="tpu_custom_call" | custom-call | tf_op jit(solution)/shard_map/panels/pallas_call | solution.py:489
  109.5 0.0 copy-done
  109.6 0.0 copy-done.1
  109.6 22.6 %update.1 = (f32[1152,2304]{1,0:T(8,128)}, f32[1152,128]{1,0:T(8,128)}) custom-call(f32[512,512]{1,0:T(8,128)S(1)} %get-tuple-element.8.a_ref, f32[512,512]{1,0:T(8,128)S(1)} %get-tuple-element.9.g_ref, f32[8,128]{1,0:T(8,128)S(1)} %get-tuple-element.10.size_ref, f32[512,1152]{1,0:T(8,128)S(1)} %bitcast.4, f32[2,512,1152]{2,1,0:T(8,128)S(1)} %bitcast.3, ...), custom_call_target="tpu_custom_call" | custom-call | tf_op jit(solution)/shard_map/update/pallas_call | solution.py:577
Async XLA Ops:
  0.6 108.9 %copy-start = (f32[1152,128]{1,0:T(8,128)S(1)}, f32[1152,128]{1,0:T(8,128)}, u32[]{:S(2)}) copy-start(f32[1152,128]{1,0:T(8,128)} %w_ref.3) | copy-start | bytes 1769476
  0.6 108.9 %copy-start.1 = (s32[512]{0:T(512)S(1)}, s32[512]{0:T(512)}, u32[]{:S(2)}) copy-start(s32[512]{0:T(512)} %param.5) | copy-start | bytes 6148

commit v9 on v8

--- a/solution.py
+++ b/solution.py
@@ -426,6 +426,7 @@
     sh2[...] = (sh[...] + rs1[2]) + (rs1[0] + rs1[1])
     s2 = copies.start(sh2, rs2, at.y_far)
     gc.own_ring()
+    gc.pair_across()
     copies.arrived(s2, rs2, at.y_far)
     s_all[k, col] = sh2[...] + rs2[...]
     gs = Gather(copies, s_all.at[k], at.y_lo, at.z, at.y_near, at.z_up, at.z_down, half)
@@ -435,7 +436,6 @@
     gs.pair_across()
     gr.forward_own()
     gc.forward_own()
-    gc.pair_across()
     for step in ((0, 3), (0, 1), (1, 0)):
         u[step] = to_sibling(*step)
     gs.far_own()

time: 134 us -> 135 us (level)
  no operation moved by 1% of the time
where the time goes in v9:
time: 135 us; the launch traced here: 132 us
  Pallas kernels  131 us (97%)
    pallas_call x1, Pallas kernels, panels(): pl.pallas_call(panels_kernel, out_shape=(jax.ShapeDtypeStruct((2, 8, CHUN...  109 us
    pallas_call x1, Pallas kernels, update(): pl.pallas_call(update_kernel, grid=(2 * BLOCKS,), out_shape=(jax.ShapeDty...  22.6 us

profile of v9, /device:TPU:0, one launch (start us, length us, event | category | flops | bytes accessed | tf_op | source)
XLA Modules:
  0.0 132.2 jit_solution(462523368475061045)
XLA Ops:
  0.6 0.0 copy-start
  0.6 0.0 copy-start.1
  0.6 108.8 %panels.1 = (f32[2,8,64,1152]{3,2,1,0:T(8,128)S(1)}, f32[8,64,1152]{2,1,0:T(8,128)S(1)}, f32[512,512]{1,0:T(8,128)S(1)}, f32[512,512]{1,0:T(8,128)S(1)}, f32[8,128]{1,0:T(8,128)S(1)}, /*index=5*/f32[512,128]{1,0:T(8,128)S(1)}) custom-call(f32[144,512]{1,0:T(8,128)} %x_ref.1, f32[1152,128]{1,0:T(8,128)} %w_ref.3, f32[1152,2304]{1,0:T(8,128)} %r_ref.3), custom_call_target="tpu_custom_call" | custom-call | tf_op jit(solution)/shard_map/panels/pallas_call | solution.py:489
  109.4 0.0 copy-done
  109.4 0.0 copy-done.1
  109.4 22.6 %update.1 = (f32[1152,2304]{1,0:T(8,128)}, f32[1152,128]{1,0:T(8,128)}) custom-call(f32[512,512]{1,0:T(8,128)S(1)} %get-tuple-element.8.a_ref, f32[512,512]{1,0:T(8,128)S(1)} %get-tuple-element.9.g_ref, f32[8,128]{1,0:T(8,128)S(1)} %get-tuple-element.10.size_ref, f32[512,1152]{1,0:T(8,128)S(1)} %bitcast.4, f32[2,512,1152]{2,1,0:T(8,128)S(1)} %bitcast.3, ...), custom_call_target="tpu_custom_call" | custom-call | tf_op jit(solution)/shard_map/update/pallas_call | solution.py:577
Async XLA Ops:
  0.6 108.8 %copy-start = (f32[1152,128]{1,0:T(8,128)S(1)}, f32[1152,128]{1,0:T(8,128)}, u32[]{:S(2)}) copy-start(f32[1152,128]{1,0:T(8,128)} %w_ref.3) | copy-start | bytes 1769476
  0.6 108.8 %copy-start.1 = (s32[512]{0:T(512)S(1)}, s32[512]{0:T(512)}, u32[]{:S(2)}) copy-start(s32[512]{0:T(512)} %param.5) | copy-start | bytes 6148
